TPU v7x, 32 devices: a whole 2x2x4 slice. The times are simulated.
32 devices in a mesh: clips: 2 (over y), row: 4 (over x, core), col: 4 (over z).
Axes of the slice: x: 2, y: 2, z: 4, core: 2. Of those that a mesh axis runs over, the one named last changes fastest.
Arguments:
- clip_tokens: bfloat16 [2048, 6144], P(('clips', 'col'), 'row'), parts along dimension 0, may hold values from -12 to 12
- modulation: float32 [8, 6, 6144], P('clips', None, 'row'), parts along dimension 0, may hold values from -3 to 3
- w_qkv: bfloat16 [6144, 3, 4096], P('row', None, 'col'), may hold values from -3 to 3
- w_out: bfloat16 [4096, 6144], P('col', 'row'), may hold values from -0.09375 to 0.09375
- w_up: bfloat16 [6144, 12288], P('row', 'col'), may hold values from -0.078125 to 0.078125
- up_bias: float32 [12288], P('col'), may hold values from -3 to 3
- w_down: bfloat16 [12288, 6144], P('col', 'row'), may hold values from -0.0546875 to 0.0546875
- guide_num: int32 [8], P('clips'), parts along dimension 0, may hold values from -3 to 10, as said below
Outputs:
- guided: bfloat16 [512, 6144], P(('clips', 'col'), 'row'), parts along dimension 0
There are 2 independent parts, one for each index of `clips`. A program takes and returns all parts, laid end to end along the dimension named above; an argument that names none is the same for every part. Nothing has to cross between parts.
Inputs may be any that keep to these rules, and one draw needn't show every extreme that they name: `guide_num`: the three negative numerators are -1, -2 and -3 in some order, and the positive one makes the four sum to 4.
All inputs are finite; a program needn't handle non-finite values.
Results may differ from a plain program's by a relative error of at most 0.019.
Values may be sent and summed in bfloat16 or wider, within the bound.
A program may use at most 128 MiB of HBM per device.

v0:
```python
import jax
import jax.numpy as jnp
from jax import lax
from jax.sharding import PartitionSpec as P

D = 6144
HEAD_DIM = 128


eps = 1e-06


def normalize(values, shift, scale):
    totals = lax.psum((jnp.sum(values, axis=1), jnp.sum(values * values, axis=1)), "row")
    mean = totals[0] / D
    variance = totals[1] / D - mean * mean
    normed = (values - mean[:, None]) * lax.rsqrt(variance + eps)[:, None]
    branches = shift.shape[0]
    shaped = normed.reshape(-1, branches, values.shape[1]) * (1.0 + scale[None]) + shift[None]
    return shaped.reshape(values.shape)


def on_device(clip_tokens, modulation, w_qkv, w_out, w_up, up_bias, w_down, guide_num):
    branches = modulation.shape[0]
    feat_rows = w_qkv.shape[0]
    head_cols = w_qkv.shape[2]
    heads_here = head_cols // HEAD_DIM
    x_rows = clip_tokens.astype(jnp.float32)
    first = normalize(x_rows, modulation[:, 0], modulation[:, 1]).astype(jnp.bfloat16)
    w_flat = w_qkv.reshape(feat_rows, 3 * head_cols)
    partial_qkv = jnp.dot(
        lax.all_gather(first, "col", axis=0, tiled=True), w_flat, preferred_element_type=jnp.float32
    )
    scale_score = 1.0 / jnp.sqrt(jnp.float32(HEAD_DIM))
    qkv = lax.psum_scatter(partial_qkv.astype(jnp.bfloat16), "row", scatter_dimension=0, tiled=True)
    query3 = qkv[:, :head_cols].reshape(-1, heads_here, HEAD_DIM)
    query_rows = query3.shape[0]
    piece = (
        lax.all_gather(qkv[:, head_cols : 2 * head_cols], "row", axis=0, tiled=True),
        lax.all_gather(qkv[:, 2 * head_cols :], "row", axis=0, tiled=True),
    )
    top = jnp.full((heads_here, query_rows), -1e30, jnp.float32)
    rows = piece[0].shape[0]
    key_heads = piece[0].reshape(rows, heads_here, HEAD_DIM)
    value_heads = piece[1].reshape(rows, heads_here, HEAD_DIM)
    scores = (
        jnp.einsum("qhd,khd->hqk", query3, key_heads, preferred_element_type=jnp.float32)
        * scale_score
    )
    query_branch = jnp.arange(query3.shape[0], dtype=jnp.int32) % branches
    key_branch = jnp.arange(rows, dtype=jnp.int32) % branches
    allowed = (query_branch[:, None] == key_branch[None, :])[None]
    masked = jnp.where(allowed, scores, -1e30)
    new_top = jnp.maximum(top, jnp.max(masked, axis=-1))
    weights = jnp.where(allowed, jnp.exp(masked - new_top[..., None]), 0.0)
    denom = jnp.sum(weights, axis=-1)
    accum = jnp.einsum(
        "hqk,khd->hqd",
        weights.astype(jnp.bfloat16),
        value_heads,
        preferred_element_type=jnp.float32,
    )
    att = (accum / denom[..., None]).transpose(1, 0, 2).reshape(-1, head_cols).astype(jnp.bfloat16)
    partial_out = jnp.dot(
        lax.all_gather(att, "row", axis=0, tiled=True), w_out, preferred_element_type=jnp.float32
    )
    out_rows = lax.psum_scatter(
        partial_out.astype(jnp.bfloat16), "col", scatter_dimension=0, tiled=True
    ).astype(jnp.float32)
    by_branch = x_rows.shape[0] // branches
    resid = (
        x_rows.reshape(by_branch, branches, feat_rows)
        + modulation[None, :, 2] * out_rows.reshape(by_branch, branches, feat_rows)
    ).reshape(x_rows.shape)
    second = normalize(resid, modulation[:, 3], modulation[:, 4]).astype(jnp.bfloat16)
    partial_up = jnp.dot(
        lax.all_gather(second, "col", axis=0, tiled=True), w_up, preferred_element_type=jnp.float32
    )
    up_rows = lax.psum_scatter(
        partial_up.astype(jnp.bfloat16), "row", scatter_dimension=0, tiled=True
    ).astype(jnp.float32)
    act = jax.nn.gelu(up_rows + up_bias[None], approximate=True).astype(jnp.bfloat16)
    partial_down = jnp.dot(
        lax.all_gather(act, "row", axis=0, tiled=True), w_down, preferred_element_type=jnp.float32
    )
    guide_weights = guide_num.astype(jnp.float32) / 4.0
    weights_gate = guide_weights[:, None] * modulation[:, 5]
    combined = jnp.sum(partial_down.reshape(-1, branches, feat_rows) * weights_gate[None], axis=1)
    mlp_rows = lax.psum_scatter(
        combined.astype(jnp.bfloat16), "col", scatter_dimension=0, tiled=True
    ).astype(jnp.float32)
    resid_mix = jnp.sum(
        resid.reshape(by_branch, branches, feat_rows) * guide_weights[None, :, None], axis=1
    )
    return (resid_mix + mlp_rows).astype(jnp.bfloat16)


def solution(mesh):
    in_specs = (
        P(("clips", "col"), "row"),
        P("clips", None, "row"),
        P("row", None, "col"),
        P("col", "row"),
        P("row", "col"),
        P("col"),
        P("col", "row"),
        P("clips"),
    )
    out_specs = P(("clips", "col"), "row")
    return jax.shard_map(
        on_device, mesh=mesh, in_specs=in_specs, out_specs=out_specs, check_vma=False
    )
```

profile of v0, /device:TPU:0, one launch (start us, length us, event | category | flops | bytes accessed | tf_op | source)
XLA Modules:
  0.0 576.2 jit_solution(1728435133668911533)
XLA Ops:
  6.5 1.6 convert_reduce_fusion
  8.2 0.8 add_bitcast_fusion
  9.0 1.4 add.126
  10.4 2.8 add.127
  13.1 1.4 mul.126
  14.5 2.8 mul.127
  17.3 8.3 %all-reduce.1 = (f32[256]{0:T(256)S(1)}, f32[256]{0:T(256)S(1)}) all-reduce(f32[256]{0:T(256)S(1)} %get-tuple-element.8, f32[256]{0:T(256)S(1)} %get-tuple-element.7), channel_id=1, replica_groups=mesh['clips'=2,'row'=4,'col'=4] {'row'}, use_global_device_ids=true, to_apply=%region_3.0 | all-reduce | flops 512 | bytes 4096 | tf_op jit(solution)/shard_map/psum | solution.py:14
  25.6 3.3 add_convert_fusion.1
  29.0 12.8 %copy.12 = bf16[1536,3,1024]{0,2,1:T(8,128)(2,1)} copy(bf16[1536,3,1024]{2,0,1:T(8,128)(2,1)} %param.10) | data formatting | bytes 18874368 | tf_op args[2]
  41.7 51.2 %all-gather.7.cloned.1.call-done = bf16[1024,1536]{1,0:T(8,128)(2,1)} async-done(((bf16[256,1536]{1,0:T(8,128)(2,1)}), bf16[1024,1536]{1,0:T(8,128)(2,1)}) %all-gather.7.cloned.1.call-update) | async-done | bytes 3145744 | tf_op jit(solution)/shard_map/all_gather | solution.py:32
  92.9 15.2 %convolution_convert_fusion.1 = bf16[1024,3072]{1,0:T(8,128)(2,1)} fusion(bf16[1024,1536]{1,0:T(8,128)(2,1)} %all-gather.7.cloned.1.call-done, bf16[1536,3072]{0,1:T(8,128)(2,1)} %bitcast.45), kind=kOutput, calls=%fused_computation.7 | convolution fusion | flops 9666822144 | bytes 18874368 | tf_op jit(solution)/shard_map/dot_general | solution.py:31
  108.2 57.1 %reduce-scatter.5.cloned.1.call-done = bf16[256,3072]{1,0:T(8,128)(2,1)} async-done(((bf16[1024,3072]{1,0:T(8,128)(2,1)}), bf16[256,3072]{1,0:T(8,128)(2,1)}) %reduce-scatter.5.cloned.1.call-update) | async-done | bytes 1572880 | tf_op jit(solution)/shard_map/reduce_scatter | solution.py:35
  165.3 2.6 slice_bitcast_fusion
  168.0 0.5 all-gather.11.cloned.1.call-update
  168.5 0.2 all-gather.13.cloned.1.call-start
  168.7 0.2 broadcast_compare_fusion
  169.0 21.7 %all-gather.9.cloned.1.call-done = bf16[1024,1024]{1,0:T(8,128)(2,1)} async-done(((bf16[256,1024]{1,0:T(8,128)(2,1)}), bf16[1024,1024]{1,0:T(8,128)(2,1)}) %all-gather.9.cloned.1.call-update) | async-done | bytes 2097168 | tf_op jit(solution)/shard_map/all_gather | solution.py:39
  190.7 3.7 fusion
  194.4 3.2 copy-done.2
  197.6 2.5 fusion.1
  200.1 14.7 %all-gather.11.cloned.1.call-done = bf16[1024,1024]{1,0:T(8,128)(2,1)} async-done(((bf16[256,1024]{1,0:T(8,128)(2,1)}), bf16[1024,1024]{1,0:T(8,128)(2,1)}) %all-gather.11.cloned.1.call-update) | async-done | bytes 2097168 | tf_op jit(solution)/shard_map/all_gather | solution.py:40
  214.8 3.9 copy.16
  218.7 7.1 %divide_convert_fusion = bf16[256,8,128]{0,2,1:T(8,128)(2,1)} fusion(bf16[1024,8,128]{0,2,1:T(8,128)(2,1)} %bitcast.46, f32[8,256,1024]{2,1,0:T(8,128)} %copy-done.2, f32[8,256]{1,0:T(8,128)S(1)} %broadcast_maximum_fusion, pred[256,1024]{1,0:T(8,128)(4,1)S(1)} %broadcast_compare_fusion, f32[256,8]{0,1:T(8,128)S(1)} %bitcast.48), kind=kOutput, calls=%fused_computation.31 | convolution fusion | flops 547880960 | bytes 11288576 | tf_op jit(solution)/shard_map/hqk,khd->hqd/dot_general | solution.py:57
  225.9 22.9 %all-gather.13.cloned.1.call-done = bf16[1024,1024]{0,1:T(8,128)(2,1)} async-done(((bf16[256,1024]{0,1:T(8,128)(2,1)}), bf16[1024,1024]{0,1:T(8,128)(2,1)}) %all-gather.13.cloned.1.call-update) | async-done | bytes 2097168 | tf_op jit(solution)/shard_map/all_gather | solution.py:65
  248.9 6.6 %convolution_convert_fusion.2 = bf16[1024,1536]{1,0:T(8,128)(2,1)} fusion(bf16[1024,1024]{0,1:T(8,128)(2,1)} %all-gather.13.cloned.1.call-done, bf16[1024,1536]{1,0:T(8,128)(2,1)S(1)} %copy-done), kind=kOutput, calls=%fused_computation.11 | convolution fusion | flops 3222798336 | bytes 8388608 | tf_op jit(solution)/shard_map/dot_general | solution.py:64
  255.8 0.5 mul.134
  256.5 1.7 add.136
  258.2 1.4 mul.140
  259.6 2.8 mul.141
  262.4 53.6 %reduce-scatter.7.cloned.1.call-done = bf16[256,1536]{1,0:T(8,128)(2,1)} async-done(((bf16[1024,1536]{1,0:T(8,128)(2,1)}), bf16[256,1536]{1,0:T(8,128)(2,1)}) %reduce-scatter.7.cloned.1.call-update) | async-done | bytes 786448 | tf_op jit(solution)/shard_map/reduce_scatter | solution.py:67
  315.9 1.7 fusion.30
  317.6 6.4 %all-reduce = (f32[256]{0:T(256)S(1)}, f32[256]{0:T(256)S(1)}) all-reduce(f32[256]{0:T(256)S(1)} %get-tuple-element.6, f32[256]{0:T(256)S(1)} %get-tuple-element.5), channel_id=1, replica_groups=mesh['clips'=2,'row'=4,'col'=4] {'row'}, use_global_device_ids=true, to_apply=%region_12.13 | all-reduce | flops 512 | bytes 4096 | tf_op jit(solution)/shard_map/psum | solution.py:14
  324.0 3.2 add_convert_fusion
  327.3 0.3 reduce-scatter.9.cloned.1.call-start
  327.5 63.0 %all-gather.15.cloned.1.call-done = bf16[1024,1536]{1,0:T(8,128)(2,1)} async-done(((bf16[256,1536]{1,0:T(8,128)(2,1)}), bf16[1024,1536]{1,0:T(8,128)(2,1)}) %all-gather.15.cloned.1.call-update) | async-done | bytes 3145744 | tf_op jit(solution)/shard_map/all_gather | solution.py:77
  390.5 15.1 %convolution_convert_fusion = bf16[1024,3072]{1,0:T(8,128)(2,1)} fusion(bf16[1024,1536]{1,0:T(8,128)(2,1)} %all-gather.15.cloned.1.call-done, bf16[1536,3072]{1,0:T(8,128)(2,1)} %param.12), kind=kOutput, calls=%fused_computation.6 | convolution fusion | flops 9666822144 | bytes 18874368 | tf_op jit(solution)/shard_map/dot_general | solution.py:76
  405.7 57.1 %reduce-scatter.9.cloned.1.call-done = bf16[256,3072]{1,0:T(8,128)(2,1)} async-done(((bf16[1024,3072]{1,0:T(8,128)(2,1)}), bf16[256,3072]{1,0:T(8,128)(2,1)}) %reduce-scatter.9.cloned.1.call-update) | async-done | bytes 1572880 | tf_op jit(solution)/shard_map/reduce_scatter | solution.py:79
  462.8 3.8 fusion.13
  466.7 0.8 bitcast_multiply_fusion
  467.5 45.7 %all-gather.17.cloned.1.call-done = bf16[1024,3072]{1,0:T(8,128)(2,1)} async-done(((bf16[256,3072]{1,0:T(8,128)(2,1)}), bf16[1024,3072]{1,0:T(8,128)(2,1)}) %all-gather.17.cloned.1.call-update) | async-done | bytes 6291472 | tf_op jit(solution)/shard_map/all_gather | solution.py:84
  513.2 15.4 %fusion.31 = f32[1024,1536]{1,0:T(8,128)} fusion(bf16[1024,3072]{1,0:T(8,128)(2,1)} %all-gather.17.cloned.1.call-done, bf16[3072,1536]{1,0:T(8,128)(2,1)} %param.14), kind=kOutput, calls=%fused_computation.59 | convolution fusion | flops 9663676416 | bytes 22020096 | tf_op jit(solution)/shard_map/dot_general | solution.py:83
  528.6 7.6 %reshape.131 = f32[256,4,1536]{2,1,0:T(4,128)} reshape(f32[1024,1536]{1,0:T(8,128)} %fusion.31) | data formatting | bytes 12582912 | tf_op jit(solution)/shard_map/reshape | solution.py:88
  536.2 8.0 %multiply_reduce_fusion = bf16[256,1536]{1,0:T(8,128)(2,1)} fusion(f32[256,4,1536]{2,1,0:T(4,128)} %reshape.131, f32[4,1536]{1,0:T(4,128)S(1)} %bitcast_multiply_fusion), kind=kLoop, calls=%fused_computation.3 | loop fusion | flops 2752512 | bytes 7102464 | tf_op jit(solution)/shard_map/reduce_sum | solution.py:88
  544.2 2.8 reshape.125
  547.0 2.6 reshape.130
  549.6 3.2 multiply_reduce_fusion.2
  552.8 14.9 %reduce-scatter.11.cloned.1.call-done = bf16[64,1536]{1,0:T(8,128)(2,1)} async-done(((bf16[256,1536]{1,0:T(8,128)(2,1)}), bf16[64,1536]{1,0:T(8,128)(2,1)}) %reduce-scatter.11.cloned.1.call-update) | async-done | bytes 196624 | tf_op jit(solution)/shard_map/reduce_scatter | solution.py:89
  567.7 1.6 add_convert_fusion.2
  (40 shorter events, 0.9 us)
Async XLA Ops:
  6.5 242.4 %copy-start = (bf16[1024,1536]{1,0:T(8,128)(2,1)S(1)}, bf16[1024,1536]{1,0:T(8,128)(2,1)}, u32[]{:S(2)}) copy-start(bf16[1024,1536]{1,0:T(8,128)(2,1)} %param.11) | copy-start | bytes 9437188
  6.5 86.4 %all-gather.7.cloned.1.call-start = ((), (), s32[]{:S(2)}) async-start(), calls=%async_computation.4 | async-start | bytes 3932160 | tf_op jit(solution)/shard_map/all_gather | solution.py:32
  9.0 246.5 %copy-start.5 = (f32[4,1536]{1,0:T(4,128)}, f32[4,1536]{1,0:T(4,128)S(1)}, u32[]{:S(2)}) copy-start(f32[4,1536]{1,0:T(4,128)S(1)} %get-tuple-element.19) | copy-start | bytes 73732
  28.9 136.4 %reduce-scatter.5.cloned.1.call-start = ((), (), s32[]{:S(2)}) async-start(), calls=%async_computation.5 | async-start | bytes 7864320 | tf_op jit(solution)/shard_map/reduce_scatter | solution.py:35
  108.2 82.5 %all-gather.9.cloned.1.call-start = ((), (), s32[]{:S(2)}) async-start(), calls=%async_computation.6 | async-start | bytes 2621440 | tf_op jit(solution)/shard_map/all_gather | solution.py:39
  167.9 46.9 %all-gather.11.cloned.1.call-start = ((), (), s32[]{:S(2)}) async-start(), calls=%async_computation.7 | async-start | bytes 2621440 | tf_op jit(solution)/shard_map/all_gather | solution.py:40
  168.5 80.4 %all-gather.13.cloned.1.call-start = ((), (), s32[]{:S(2)}) async-start(), calls=%async_computation.8 | async-start | bytes 2621440 | tf_op jit(solution)/shard_map/all_gather | solution.py:65
  194.3 3.2 copy-start.2
  225.9 90.0 %reduce-scatter.7.cloned.1.call-start = ((), (), s32[]{:S(2)}) async-start(), calls=%async_computation.9 | async-start | bytes 3932160 | tf_op jit(solution)/shard_map/reduce_scatter | solution.py:67
  255.5 135.0 %all-gather.15.cloned.1.call-start = ((), (), s32[]{:S(2)}) async-start(), calls=%async_computation.10 | async-start | bytes 3932160 | tf_op jit(solution)/shard_map/all_gather | solution.py:77
  258.2 57.7 %copy-start.3 = (bf16[256,1536]{1,0:T(8,128)(2,1)S(1)}, bf16[256,1536]{1,0:T(8,128)(2,1)}, u32[]{:S(2)}) copy-start(bf16[256,1536]{1,0:T(8,128)(2,1)} %param.8) | copy-start | bytes 2359300
  315.9 8.1 %copy-start.4 = (bf16[256,1536]{1,0:T(8,128)(2,1)S(1)}, bf16[256,1536]{1,0:T(8,128)(2,1)}, u32[]{:S(2)}) copy-start(bf16[256,1536]{1,0:T(8,128)(2,1)} %reduce-scatter.7.cloned.1.call-done) | copy-start | bytes 2359300
  327.3 135.5 %reduce-scatter.9.cloned.1.call-start = ((), (), s32[]{:S(2)}) async-start(), calls=%async_computation.11 | async-start | bytes 7864320 | tf_op jit(solution)/shard_map/reduce_scatter | solution.py:79
  405.6 57.2 %copy-start.6 = (f32[3072]{0:T(1024)S(1)}, f32[3072]{0:T(1024)}, u32[]{:S(2)}) copy-start(f32[3072]{0:T(1024)} %param.13) | copy-start | bytes 36868
  405.6 61.0 %copy-start.7 = (s32[4]{0:T(128)S(1)}, s32[4]{0:T(128)}, u32[]{:S(2)}) copy-start(s32[4]{0:T(128)} %param.15) | copy-start | bytes 52
  405.7 107.6 %all-gather.17.cloned.1.call-start = ((), (), s32[]{:S(2)}) async-start(), calls=%async_computation.12 | async-start | bytes 7864320 | tf_op jit(solution)/shard_map/all_gather | solution.py:84
  466.6 101.0 %reduce-scatter.11.cloned.1.call-start = ((), (), s32[]{:S(2)}) async-start(), calls=%async_computation.13 | async-start | bytes 983040 | tf_op jit(solution)/shard_map/reduce_scatter | solution.py:89
  544.2 25.1 %copy-start.1 = (bf16[1024,1536]{1,0:T(8,128)(2,1)S(1)}, bf16[1024,1536]{1,0:T(8,128)(2,1)}, u32[]{:S(2)}) copy-start(bf16[1024,1536]{1,0:T(8,128)(2,1)} %param.11) | copy-start | bytes 9437188
Sparse Core Ops, SparseCore 0:
  29.1 63.8 all-gather.6
  108.3 56.9 reduce-scatter.4
  168.0 22.5 all-gather.8
  192.2 22.5 all-gather.10
  226.0 22.8 all-gather.12
  255.6 60.2 reduce-scatter.6
  327.4 63.0 all-gather.14
  405.8 56.9 reduce-scatter.8
  466.8 46.4 all-gather.16
  544.3 23.2 reduce-scatter.10
where the time goes:
time: 577 us; the launch traced here: 576 us
  waiting for transfers between devices  402 us (70%)
  matrix products  63.2 us (11%)
  local copies, waits for them, and re-layouts  50.5 us (9%)
  other arithmetic  30.9 us (5%)
  blocking collectives  14.7 us (3%)
  between operations  13.7 us (2%)
    all_gather x1, waiting for transfers between devices, on_device(): lax.all_gather(second, 'col', axis=0, tiled=True)  63 us
    reduce_scatter x1, waiting for transfers between devices, on_device(): lax.psum_scatter(partial_up.astype(jnp.bfloat16), 'row', scatter_dimensio...  57.1 us
    reduce_scatter x1, waiting for transfers between devices, on_device(): lax.psum_scatter(partial_qkv.astype(jnp.bfloat16), 'row', scatter_dimensi...  57.1 us
    reduce_scatter x1, waiting for transfers between devices, on_device(): lax.psum_scatter(partial_out.astype(jnp.bfloat16), 'col', scatter_dimensi...  53.6 us
    all_gather x1, waiting for transfers between devices, on_device(): lax.all_gather(first, 'col', axis=0, tiled=True)  51.2 us
    all_gather x1, waiting for transfers between devices, on_device(): lax.all_gather(act, 'row', axis=0, tiled=True)  45.7 us
    all_gather x1, waiting for transfers between devices, on_device(): lax.all_gather(att, 'row', axis=0, tiled=True)  22.9 us
    all_gather x1, waiting for transfers between devices, on_device(): lax.all_gather(qkv[:, head_cols:2 * head_cols], 'row', axis=0, tiled=True)  21.7 us
  transfers between devices with their start and end apart: 10, of which 10 were waited for; matrix products, arithmetic and copies ran while one was open for 6% of the time, Pallas kernels for 0%

commit v1 on v0

--- a/solution.py
+++ b/solution.py
@@ -20,7 +20,7 @@
     return shaped.reshape(values.shape)
 
 
-def on_device(clip_tokens, modulation, w_qkv, w_out, w_up, up_bias, w_down, guide_num):
+def general_layer(clip_tokens, modulation, w_qkv, w_out, w_up, up_bias, w_down, guide_num):
     branches = modulation.shape[0]
     feat_rows = w_qkv.shape[0]
     head_cols = w_qkv.shape[2]
@@ -95,6 +95,114 @@
     return (resid_mix + mlp_rows).astype(jnp.bfloat16)
 
 
+BF = jnp.bfloat16
+
+
+def swap_row(value, distance):
+    size = lax.axis_size("row")
+    return lax.ppermute(value, "row", [(r, r ^ distance) for r in range(size)])
+
+
+def sum_over_row(value):
+    value = value + swap_row(value, 1)
+    return value + swap_row(value, 2)
+
+
+def scatter_row(pieces):
+    me = lax.axis_index("row")
+    half, core = me // 2, me % 2
+    mine = lax.dynamic_index_in_dim(pieces, core, 1, keepdims=False)
+    theirs = lax.dynamic_index_in_dim(pieces, 1 - core, 1, keepdims=False)
+    got = swap_row(theirs, 1)
+    away = lax.dynamic_index_in_dim(mine, 1 - half, 0, keepdims=False).astype(
+        jnp.float32
+    ) + lax.dynamic_index_in_dim(got, 1 - half, 0, keepdims=False).astype(jnp.float32)
+    came = swap_row(away.astype(BF), 2)
+    kept = lax.dynamic_index_in_dim(mine, half, 0, keepdims=False).astype(
+        jnp.float32
+    ) + lax.dynamic_index_in_dim(got, half, 0, keepdims=False).astype(jnp.float32)
+    return kept + came.astype(jnp.float32)
+
+
+def gather_row(value):
+    me = lax.axis_index("row")
+    half, core = me // 2, me % 2
+    other = swap_row(value, 2)
+    pair = jnp.where(half == 0, jnp.stack([value, other]), jnp.stack([other, value]))
+    beside = swap_row(pair, 1)
+    return jnp.where(
+        core == 0, jnp.stack([pair, beside], axis=1), jnp.stack([beside, pair], axis=1)
+    )
+
+
+def moments(values):
+    return jnp.stack([jnp.sum(values, axis=1), jnp.sum(values * values, axis=1)])
+
+
+def apply_norm(values, totals, shift, scale):
+    mean = totals[0] / D
+    variance = totals[1] / D - mean * mean
+    normed = (values - mean[:, None]) * lax.rsqrt(variance + eps)[:, None]
+    return (normed * (1.0 + scale[None]) + shift[None]).astype(BF)
+
+
+def attend(q, k, v):
+    scores = jnp.einsum("qhd,khd->hqk", q, k, preferred_element_type=jnp.float32)
+    scores = scores / jnp.sqrt(jnp.float32(HEAD_DIM))
+    weights = jnp.exp(scores - jnp.max(scores, axis=-1, keepdims=True))
+    denom = jnp.sum(weights, axis=-1)
+    mixed = jnp.einsum(
+        "hqk,khd->hqd", weights.astype(BF), v, preferred_element_type=jnp.float32
+    )
+    mixed = mixed / denom[..., None]
+    return mixed.transpose(1, 0, 2).reshape(q.shape[0], -1).astype(BF)
+
+
+def branch_layer(clip_tokens, modulation, w_qkv, w_out, w_up, up_bias, w_down, guide_num):
+    branches = modulation.shape[0]
+    feat_rows, _, head_cols = w_qkv.shape
+    here = clip_tokens.shape[0] // branches
+    w_flat = w_qkv.reshape(feat_rows, 3 * head_cols)
+    by_branch = clip_tokens.reshape(here, branches, feat_rows).transpose(1, 0, 2)
+    mine = head_cols // 4
+    guide = guide_num.astype(jnp.float32) / 4.0
+    total = None
+    mixed = None
+    for b in range(branches):
+        x = by_branch[b]
+        x_all = lax.all_gather(x, "col", axis=0, tiled=True).astype(jnp.float32)
+        tokens = x_all.shape[0]
+        first = apply_norm(x_all, sum_over_row(moments(x_all)), modulation[b, 0], modulation[b, 1])
+        partial = jnp.dot(first, w_flat, preferred_element_type=jnp.float32).astype(BF)
+        pieces = partial.reshape(tokens, 3, 2, 2, mine).transpose(2, 3, 1, 0, 4)
+        qkv = scatter_row(pieces).astype(BF).reshape(3, tokens, mine // HEAD_DIM, HEAD_DIM)
+        att = attend(qkv[0], qkv[1], qkv[2])
+        att_all = gather_row(att).reshape(4, tokens, mine).transpose(1, 0, 2).reshape(tokens, -1)
+        partial = jnp.dot(att_all, w_out, preferred_element_type=jnp.float32).astype(BF)
+        out = lax.psum_scatter(partial, "col", scatter_dimension=0, tiled=True)
+        resid = x.astype(jnp.float32) + modulation[b, 2][None] * out.astype(jnp.float32)
+        second = apply_norm(resid, sum_over_row(moments(resid)), modulation[b, 3], modulation[b, 4])
+        second_all = lax.all_gather(second, "col", axis=0, tiled=True)
+        partial = jnp.dot(second_all, w_up, preferred_element_type=jnp.float32).astype(BF)
+        up = scatter_row(partial.reshape(2, 2, tokens // 4, -1))
+        act = jax.nn.gelu(up + up_bias[None], approximate=True).astype(BF)
+        act_all = gather_row(act).reshape(tokens, -1)
+        down = jnp.dot(act_all, w_down, preferred_element_type=jnp.float32)
+        down = down * (guide[b] * modulation[b, 5])[None]
+        total = down if total is None else total + down
+        part = guide[b] * resid
+        mixed = part if mixed is None else mixed + part
+    mlp = lax.psum_scatter(total.astype(BF), "col", scatter_dimension=0, tiled=True)
+    return (mixed + mlp.astype(jnp.float32)).astype(BF)
+
+
+def on_device(*args):
+    heads_here = args[2].shape[2] // HEAD_DIM
+    if lax.axis_size("row") == 4 and heads_here % 4 == 0:
+        return branch_layer(*args)
+    return general_layer(*args)
+
+
 def solution(mesh):
     in_specs = (
         P(("clips", "col"), "row"),

time: 577 us -> 580 us (level)
  waiting for transfers between devices: 402 us -> 151 us
  blocking collectives: 14.7 us -> 148 us
  local copies, waits for them, and re-layouts: 50.5 us -> 101 us
  starting transfers between devices: 0.78 us -> 30.1 us
  matrix products: 63.2 us -> 89 us
  other arithmetic: 30.9 us -> 40.9 us
    all_gather x6 -> x0, waiting for transfers between devices: 219 us -> none  [the longest x1 63 us: on_device(): lax.all_gather(second, 'col', axis=0, tiled=True)]
    all_gather x0 -> x8, blocking collectives: none -> 148 us  [the longest x4 75.8 us: branch_layer(): x_all = lax.all_gather(x, 'col', axis=0, tiled=True).astype(jnp.float32)]
    reduce_scatter x4 -> x5, waiting for transfers between devices: 183 us -> 55.5 us  [the longest x4 33.3 us: branch_layer(): out = lax.psum_scatter(partial, 'col', scatter_dimension=0, tiled=True)]
    ppermute x0 -> x48, waiting for transfers between devices: none -> 95.5 us  [swap_row(): return lax.ppermute(value, 'row', [(r, r ^ distance) for r in range(size)])]
    ppermute x0 -> x48, starting transfers between devices: none -> 30 us  [swap_row(): return lax.ppermute(value, 'row', [(r, r ^ distance) for r in range(size)])]
    dot_general x6 -> x24, matrix products: 63.2 us -> 89 us  [the longest x4 40.9 us: branch_layer(): jnp.dot(first, w_flat, preferred_element_type=jnp.float32).astype(BF)]
    slice x0 -> x18, local copies, waits for them, and re-layouts: none -> 16.6 us  [the longest x16 15.9 us: branch_layer(): att = attend(qkv[0], qkv[1], qkv[2])]
    psum x2 -> x0, blocking collectives: 14.7 us -> none  [normalize(): lax.psum((jnp.sum(values, axis=1), jnp.sum(values * values, axis=1)), 'row')]
  transfers between devices with their start and end apart: 10 -> 53, of which waited for: 10 -> 22; matrix products, arithmetic and copies ran while one was open for 6% -> 34% of each run, Pallas kernels for 0% -> 0%
where the time goes in v1:
time: 580 us; the launch traced here: 575 us
  waiting for transfers between devices  151 us (26%)
  blocking collectives  148 us (26%)
  local copies, waits for them, and re-layouts  101 us (17%)
  matrix products  89 us (15%)
  other arithmetic  40.9 us (7%)
  starting transfers between devices  30.1 us (5%)
  between operations  14.7 us (3%)
    ppermute x48, waiting for transfers between devices, swap_row(): return lax.ppermute(value, 'row', [(r, r ^ distance) for r in range(size)])  95.5 us
    all_gather x4, blocking collectives, branch_layer(): x_all = lax.all_gather(x, 'col', axis=0, tiled=True).astype(jnp.float32)  75.8 us
    all_gather x4, blocking collectives, branch_layer(): second_all = lax.all_gather(second, 'col', axis=0, tiled=True)  72.7 us
    dot_general x4, matrix products, branch_layer(): jnp.dot(first, w_flat, preferred_element_type=jnp.float32).astype(BF)  40.9 us
    reduce_scatter x4, waiting for transfers between devices, branch_layer(): out = lax.psum_scatter(partial, 'col', scatter_dimension=0, tiled=True)  33.3 us
    ppermute x48, starting transfers between devices, swap_row(): return lax.ppermute(value, 'row', [(r, r ^ distance) for r in range(size)])  30 us
    reduce_scatter x1, waiting for transfers between devices, branch_layer(): lax.psum_scatter(total.astype(BF), 'col', scatter_dimension=0, tiled=True)  22.2 us
    unnamed x111, local copies, waits for them, and re-layouts  21.5 us
  transfers between devices with their start and end apart: 53, of which 22 were waited for; matrix products, arithmetic and copies ran while one was open for 34% of the time, Pallas kernels for 0%

profile of v1, /device:TPU:0, one launch (start us, length us, event | category | flops | bytes accessed | tf_op | source)
XLA Modules:
  0.0 575.2 jit_solution(8317175544174087421)
XLA Ops:
  10.4 21.3 %all-gather.3 = bf16[1,256,1536]{2,1,0:T(8,128)(2,1)S(1)} all-gather(bf16[1,64,1536]{2,1,0:T(8,128)(2,1)S(1)} %get-tuple-element.56), channel_id=5, replica_groups=mesh['clips'=2,'row'=4,'col'=4] {'col'}, dimensions={1}, use_global_device_ids=true | all-gather | bytes 983040 | tf_op jit(solution)/shard_map/all_gather | solution.py:173
  32.2 18.0 %all-gather.2 = bf16[1,256,1536]{2,1,0:T(8,128)(2,1)S(1)} all-gather(bf16[1,64,1536]{2,1,0:T(8,128)(2,1)S(1)} %get-tuple-element.55), channel_id=4, replica_groups=mesh['clips'=2,'row'=4,'col'=4] {'col'}, dimensions={1}, use_global_device_ids=true | all-gather | bytes 983040 | tf_op jit(solution)/shard_map/all_gather | solution.py:173
  51.1 18.1 %all-gather.1 = bf16[1,256,1536]{2,1,0:T(8,128)(2,1)S(1)} all-gather(bf16[1,64,1536]{2,1,0:T(8,128)(2,1)S(1)} %get-tuple-element.57), channel_id=3, replica_groups=mesh['clips'=2,'row'=4,'col'=4] {'col'}, dimensions={1}, use_global_device_ids=true | all-gather | bytes 983040 | tf_op jit(solution)/shard_map/all_gather | solution.py:173
  70.2 18.4 %all-gather = bf16[1,256,1536]{2,1,0:T(8,128)(2,1)S(1)} all-gather(bf16[1,64,1536]{2,1,0:T(8,128)(2,1)S(1)} %get-tuple-element.58), channel_id=2, replica_groups=mesh['clips'=2,'row'=4,'col'=4] {'col'}, dimensions={1}, use_global_device_ids=true | all-gather | bytes 983040 | tf_op jit(solution)/shard_map/all_gather | solution.py:173
  91.8 2.7 multiply_reduce_fusion.7
  94.5 12.7 %copy.38 = bf16[1536,3,1024]{0,2,1:T(8,128)(2,1)} copy(bf16[1536,3,1024]{2,0,1:T(8,128)(2,1)} %param.10) | data formatting | bytes 18874368 | tf_op args[2]
  111.6 7.8 %convolution_convert_fusion.4 = bf16[256,3072]{1,0:T(8,128)(2,1)} fusion(bf16[1536,3072]{0,1:T(8,128)(2,1)} %bitcast.477, bf16[1,256,1536]{2,1,0:T(8,128)(2,1)} %copy-done.14, f32[1536]{0:T(1024)S(1)} %get-tuple-element.29, f32[1536]{0:T(1024)S(1)} %get-tuple-element.30, f32[256]{0:T(256)S(1)} %add_rsqrt_fusion, f32[256]{0:T(256)S(1)} %bitcast.609), kind=kOutput, calls=%fused_computation.4 | convolution fusion | flops 2419064832 | bytes 11810816 | tf_op jit(solution)/shard_map/dot_general | solution.py:176
  119.5 5.0 reshape.1011
  124.5 3.0 constant_dynamic-slice_fusion.1
  128.8 11.0 %convolution_convert_fusion.5 = bf16[256,3072]{1,0:T(8,128)(2,1)} fusion(bf16[1536,3072]{0,1:T(8,128)(2,1)} %bitcast.478, bf16[1,256,1536]{2,1,0:T(8,128)(2,1)S(1)} %copy-done.13, f32[1536]{0:T(1024)S(1)} %get-tuple-element.32, f32[1536]{0:T(1024)S(1)} %get-tuple-element.33, f32[256]{0:T(256)S(1)} %add_rsqrt_fusion.1, f32[256]{0:T(256)S(1)} %bitcast.611), kind=kOutput, calls=%fused_computation.5 | convolution fusion | flops 2419064832 | bytes 11810816 | tf_op jit(solution)/shard_map/dot_general | solution.py:176
  139.8 5.2 reshape.1009
  145.1 3.0 constant_dynamic-slice_fusion.4
  149.5 11.0 %convolution_convert_fusion.6 = bf16[256,3072]{1,0:T(8,128)(2,1)} fusion(bf16[1536,3072]{0,1:T(8,128)(2,1)} %bitcast.479, bf16[1,256,1536]{2,1,0:T(8,128)(2,1)S(1)} %copy-done.11, f32[1536]{0:T(1024)S(1)} %get-tuple-element.36, f32[1536]{0:T(1024)S(1)} %get-tuple-element.37, f32[256]{0:T(256)S(1)} %add_rsqrt_fusion.2, f32[256]{0:T(256)S(1)} %bitcast.613), kind=kOutput, calls=%fused_computation.6 | convolution fusion | flops 2419064832 | bytes 11810816 | tf_op jit(solution)/shard_map/dot_general | solution.py:176
  160.5 5.0 reshape.1007
  165.5 3.0 constant_dynamic-slice_fusion.7
  169.8 11.0 %convolution_convert_fusion.7 = bf16[256,3072]{1,0:T(8,128)(2,1)} fusion(bf16[1536,3072]{0,1:T(8,128)(2,1)} %bitcast.480, bf16[1,256,1536]{2,1,0:T(8,128)(2,1)S(1)} %copy-done.9, f32[1536]{0:T(1024)S(1)} %get-tuple-element.39, f32[1536]{0:T(1024)S(1)} %get-tuple-element.40, f32[256]{0:T(256)S(1)} %add_rsqrt_fusion.3, f32[256]{0:T(256)S(1)} %bitcast.607), kind=kOutput, calls=%fused_computation.7 | convolution fusion | flops 2419064832 | bytes 11810816 | tf_op jit(solution)/shard_map/dot_general | solution.py:176
  180.9 5.5 reshape.1005
  186.3 3.0 constant_dynamic-slice_fusion.10
  209.9 3.2 collective-permute-done.21
  226.4 14.1 %collective-permute-done.22 = bf16[256,256]{1,0:T(8,128)(2,1)S(1)} collective-permute-done((bf16[256,256]{1,0:T(8,128)(2,1)}, bf16[256,256]{1,0:T(8,128)(2,1)S(1)}, u32[]{:S(2)}, u32[]{:S(2)}) %collective-permute-start.22) | collective-permute-done | bytes 131104 | tf_op jit(solution)/shard_map/ppermute | solution.py:103
  249.4 3.1 convolution_convert_fusion.8
  272.4 3.0 convolution_convert_fusion.9
  296.4 3.0 convolution_convert_fusion.10
  302.9 4.5 collective-permute-done.4
  314.0 3.0 convolution_convert_fusion.11
  317.1 8.5 %reduce-scatter.8.cloned.1.call-done = bf16[64,1536]{1,0:T(8,128)(2,1)} async-done(((bf16[256,1536]{1,0:T(8,128)(2,1)}), bf16[64,1536]{1,0:T(8,128)(2,1)}) %reduce-scatter.8.cloned.1.call-update) | async-done | bytes 196624 | tf_op jit(solution)/shard_map/reduce_scatter | solution.py:182
  325.6 24.8 %reduce-scatter.6.cloned.1.call-done = bf16[64,1536]{1,0:T(8,128)(2,1)} async-done(((bf16[256,1536]{1,0:T(8,128)(2,1)}), bf16[64,1536]{1,0:T(8,128)(2,1)}) %reduce-scatter.6.cloned.1.call-update) | async-done | bytes 196624 | tf_op jit(solution)/shard_map/reduce_scatter | solution.py:182
  361.4 18.1 %all_gather.31 = bf16[256,1536]{1,0:T(8,128)(2,1)S(1)} all-gather(bf16[64,1536]{1,0:T(8,128)(2,1)S(1)} %get-tuple-element.54), channel_id=1, replica_groups=mesh['clips'=2,'row'=4,'col'=4] {'col'}, dimensions={0}, use_global_device_ids=true | all-gather | bytes 983040 | tf_op jit(solution)/shard_map/all_gather | solution.py:185
  379.5 6.4 %convolution_convert_fusion = bf16[256,3072]{1,0:T(8,128)(2,1)S(1)} fusion(bf16[256,1536]{1,0:T(8,128)(2,1)S(1)} %all_gather.31, bf16[1536,3072]{1,0:T(8,128)(2,1)} %param.12), kind=kOutput, calls=%fused_computation | convolution fusion | flops 2416705536 | bytes 11796480 | tf_op jit(solution)/shard_map/dot_general | solution.py:186
  387.3 18.0 %all_gather.30 = bf16[256,1536]{1,0:T(8,128)(2,1)S(1)} all-gather(bf16[64,1536]{1,0:T(8,128)(2,1)S(1)} %get-tuple-element.52), channel_id=1, replica_groups=mesh['clips'=2,'row'=4,'col'=4] {'col'}, dimensions={0}, use_global_device_ids=true | all-gather | bytes 983040 | tf_op jit(solution)/shard_map/all_gather | solution.py:185
  405.3 2.6 convolution_convert_fusion.1
  408.1 18.2 %all_gather.29 = bf16[256,1536]{1,0:T(8,128)(2,1)S(1)} all-gather(bf16[64,1536]{1,0:T(8,128)(2,1)S(1)} %get-tuple-element.53), channel_id=1, replica_groups=mesh['clips'=2,'row'=4,'col'=4] {'col'}, dimensions={0}, use_global_device_ids=true | all-gather | bytes 983040 | tf_op jit(solution)/shard_map/all_gather | solution.py:185
  426.3 2.6 convolution_convert_fusion.2
  429.1 18.4 %all_gather.28 = bf16[256,1536]{1,0:T(8,128)(2,1)S(1)} all-gather(bf16[64,1536]{1,0:T(8,128)(2,1)S(1)} %get-tuple-element.51), channel_id=1, replica_groups=mesh['clips'=2,'row'=4,'col'=4] {'col'}, dimensions={0}, use_global_device_ids=true | all-gather | bytes 983040 | tf_op jit(solution)/shard_map/all_gather | solution.py:185
  455.0 7.3 %collective-permute-done.45 = bf16[64,3072]{1,0:T(8,128)(2,1)S(1)} collective-permute-done((bf16[64,3072]{1,0:T(8,128)(2,1)S(1)}, bf16[64,3072]{1,0:T(8,128)(2,1)S(1)}, u32[]{:S(2)}, u32[]{:S(2)}) %collective-permute-start.45) | collective-permute-done | bytes 393248 | tf_op jit(solution)/shard_map/ppermute | solution.py:103
  462.3 8.4 %collective-permute-done.39 = bf16[64,3072]{1,0:T(8,128)(2,1)S(1)} collective-permute-done((bf16[64,3072]{1,0:T(8,128)(2,1)S(1)}, bf16[64,3072]{1,0:T(8,128)(2,1)S(1)}, u32[]{:S(2)}, u32[]{:S(2)}) %collective-permute-start.39) | collective-permute-done | bytes 393248 | tf_op jit(solution)/shard_map/ppermute | solution.py:103
  470.7 8.4 %collective-permute-done.33 = bf16[64,3072]{1,0:T(8,128)(2,1)S(1)} collective-permute-done((bf16[64,3072]{1,0:T(8,128)(2,1)S(1)}, bf16[64,3072]{1,0:T(8,128)(2,1)S(1)}, u32[]{:S(2)}, u32[]{:S(2)}) %collective-permute-start.33) | collective-permute-done | bytes 393248 | tf_op jit(solution)/shard_map/ppermute | solution.py:103
  479.1 8.0 %collective-permute-done.27 = bf16[64,3072]{1,0:T(8,128)(2,1)S(1)} collective-permute-done((bf16[64,3072]{1,0:T(8,128)(2,1)S(1)}, bf16[64,3072]{1,0:T(8,128)(2,1)S(1)}, u32[]{:S(2)}, u32[]{:S(2)}) %collective-permute-start.27) | collective-permute-done | bytes 393248 | tf_op jit(solution)/shard_map/ppermute | solution.py:103
  492.9 8.0 %collective-permute-done.28 = bf16[64,3072]{1,0:T(8,128)(2,1)S(1)} collective-permute-done((bf16[64,3072]{1,0:T(8,128)(2,1)S(1)}, bf16[64,3072]{1,0:T(8,128)(2,1)S(1)}, u32[]{:S(2)}, u32[]{:S(2)}) %collective-permute-start.28) | collective-permute-done | bytes 393248 | tf_op jit(solution)/shard_map/ppermute | solution.py:103
  501.1 8.2 %collective-permute-done.34 = bf16[64,3072]{1,0:T(8,128)(2,1)S(1)} collective-permute-done((bf16[64,3072]{1,0:T(8,128)(2,1)S(1)}, bf16[64,3072]{1,0:T(8,128)(2,1)S(1)}, u32[]{:S(2)}, u32[]{:S(2)}) %collective-permute-start.34) | collective-permute-done | bytes 393248 | tf_op jit(solution)/shard_map/ppermute | solution.py:103
  509.5 8.2 %collective-permute-done.40 = bf16[64,3072]{1,0:T(8,128)(2,1)S(1)} collective-permute-done((bf16[64,3072]{1,0:T(8,128)(2,1)S(1)}, bf16[64,3072]{1,0:T(8,128)(2,1)S(1)}, u32[]{:S(2)}, u32[]{:S(2)}) %collective-permute-start.40) | collective-permute-done | bytes 393248 | tf_op jit(solution)/shard_map/ppermute | solution.py:103
  517.9 6.9 %collective-permute-done.46 = bf16[64,3072]{1,0:T(8,128)(2,1)S(1)} collective-permute-done((bf16[64,3072]{1,0:T(8,128)(2,1)S(1)}, bf16[64,3072]{1,0:T(8,128)(2,1)S(1)}, u32[]{:S(2)}, u32[]{:S(2)}) %collective-permute-start.46) | collective-permute-done | bytes 393248 | tf_op jit(solution)/shard_map/ppermute | solution.py:103
  529.5 2.6 convolution_multiply_fusion.2
  532.1 2.6 convolution_multiply_fusion.1
  534.8 2.9 convolution_multiply_fusion
  537.7 3.5 fusion.3
  541.3 22.2 %reduce-scatter.14.cloned.1.call-done = bf16[64,1536]{1,0:T(8,128)(2,1)} async-done(((bf16[256,1536]{1,0:T(8,128)(2,1)}), bf16[64,1536]{1,0:T(8,128)(2,1)}) %reduce-scatter.14.cloned.1.call-update) | async-done | bytes 196624 | tf_op jit(solution)/shard_map/reduce_scatter | solution.py:195
  563.5 4.9 add_convert_fusion
  (362 shorter events, 141.9 us)
Async XLA Ops:
  6.5 310.5 %reduce-scatter.12.cloned.1.call-start = ((), (), s32[]{:S(2)}) async-start(), calls=%async_computation.8 | async-start | bytes 983040 | tf_op jit(solution)/shard_map/reduce_scatter | solution.py:182
  32.1 75.1 %collective-permute-start.18 = (f32[2,256]{1,0:T(2,128)S(1)}, f32[2,256]{1,0:T(2,128)S(1)}, u32[]{:S(2)}, u32[]{:S(2)}) collective-permute-start(f32[2,256]{1,0:T(2,128)S(1)} %pad_maximum_fusion.3), channel_id=1, source_target_pairs={{0,4},{4,0},{8,12},{12,8},{1,5},{5,1},{9,13},{13,9},{2,6},{6,2},{1... | collective-permute-start | bytes 6152 | tf_op jit(solution)/shard_map/ppermute | solution.py:103
  50.6 58.2 %collective-permute-start.12 = (f32[2,256]{1,0:T(2,128)S(1)}, f32[2,256]{1,0:T(2,128)S(1)}, u32[]{:S(2)}, u32[]{:S(2)}) collective-permute-start(f32[2,256]{1,0:T(2,128)S(1)} %pad_maximum_fusion.2), channel_id=1, source_target_pairs={{0,4},{4,0},{8,12},{12,8},{1,5},{5,1},{9,13},{13,9},{2,6},{6,2},{1... | collective-permute-start | bytes 6152 | tf_op jit(solution)/shard_map/ppermute | solution.py:103
  69.7 39.7 %collective-permute-start.6 = (f32[2,256]{1,0:T(2,128)S(1)}, f32[2,256]{1,0:T(2,128)S(1)}, u32[]{:S(2)}, u32[]{:S(2)}) collective-permute-start(f32[2,256]{1,0:T(2,128)S(1)} %pad_maximum_fusion.1), channel_id=1, source_target_pairs={{0,4},{4,0},{8,12},{12,8},{1,5},{5,1},{9,13},{13,9},{2,6},{6,2},{1... | collective-permute-start | bytes 6152 | tf_op jit(solution)/shard_map/ppermute | solution.py:103
  89.7 21.3 %collective-permute-start = (f32[2,256]{1,0:T(2,128)S(1)}, f32[2,256]{1,0:T(2,128)S(1)}, u32[]{:S(2)}, u32[]{:S(2)}) collective-permute-start(f32[2,256]{1,0:T(2,128)S(1)} %pad_maximum_fusion), channel_id=1, source_target_pairs={{0,4},{4,0},{8,12},{12,8},{1,5},{5,1},{9,13},{13,9},{2,6},{6,2},{1... | collective-permute-start | bytes 6152 | tf_op jit(solution)/shard_map/ppermute | solution.py:103
  107.2 4.4 collective-permute-start.19
  108.8 19.7 %collective-permute-start.13 = (f32[2,256]{1,0:T(2,128)S(1)}, f32[2,256]{1,0:T(2,128)S(1)}, u32[]{:S(2)}, u32[]{:S(2)}) collective-permute-start(f32[2,256]{1,0:T(2,128)S(1)} %fusion.152), channel_id=1, source_target_pairs={{0,8},{4,12},{8,0},{12,4},{1,9},{5,13},{9,1},{13,5},{2,10},{6,14},... | collective-permute-start | bytes 6152 | tf_op jit(solution)/shard_map/ppermute | solution.py:103
  109.4 40.0 %collective-permute-start.7 = (f32[2,256]{1,0:T(2,128)S(1)}, f32[2,256]{1,0:T(2,128)S(1)}, u32[]{:S(2)}, u32[]{:S(2)}) collective-permute-start(f32[2,256]{1,0:T(2,128)S(1)} %fusion.153), channel_id=1, source_target_pairs={{0,8},{4,12},{8,0},{12,4},{1,9},{5,13},{9,1},{13,5},{2,10},{6,14},... | collective-permute-start | bytes 6152 | tf_op jit(solution)/shard_map/ppermute | solution.py:103
  111.0 58.8 %collective-permute-start.1 = (f32[2,256]{1,0:T(2,128)S(1)}, f32[2,256]{1,0:T(2,128)S(1)}, u32[]{:S(2)}, u32[]{:S(2)}) collective-permute-start(f32[2,256]{1,0:T(2,128)S(1)} %fusion.154), channel_id=1, source_target_pairs={{0,8},{4,12},{8,0},{12,4},{1,9},{5,13},{9,1},{13,5},{2,10},{6,14},... | collective-permute-start | bytes 6152 | tf_op jit(solution)/shard_map/ppermute | solution.py:103
  128.5 71.5 %collective-permute-start.20 = (bf16[2,3,256,256]{3,2,1,0:T(8,128)(2,1)}, bf16[2,3,256,256]{3,2,1,0:T(8,128)(2,1)}, u32[]{:S(2)}, u32[]{:S(2)}) collective-permute-start(bf16[2,3,256,256]{3,2,1,0:T(8,128)(2,1)} %bitcast.467), channel_id=1, source_target_pairs={{0,4},{4,0},{8,12},{12,8},{1,5},{5,1},{9,13},{13,9},{2,6},{6,2},{1... | collective-permute-start | bytes 2359304 | tf_op jit(solution)/shard_map/ppermute | solution.py:103
  149.1 53.5 %collective-permute-start.14 = (bf16[2,3,256,256]{3,2,1,0:T(8,128)(2,1)}, bf16[2,3,256,256]{3,2,1,0:T(8,128)(2,1)}, u32[]{:S(2)}, u32[]{:S(2)}) collective-permute-start(bf16[2,3,256,256]{3,2,1,0:T(8,128)(2,1)} %bitcast.468), channel_id=1, source_target_pairs={{0,4},{4,0},{8,12},{12,8},{1,5},{5,1},{9,13},{13,9},{2,6},{6,2},{1... | collective-permute-start | bytes 2359304 | tf_op jit(solution)/shard_map/ppermute | solution.py:103
  169.6 35.5 %collective-permute-start.8 = (bf16[2,3,256,256]{3,2,1,0:T(8,128)(2,1)}, bf16[2,3,256,256]{3,2,1,0:T(8,128)(2,1)}, u32[]{:S(2)}, u32[]{:S(2)}) collective-permute-start(bf16[2,3,256,256]{3,2,1,0:T(8,128)(2,1)} %bitcast.469), channel_id=1, source_target_pairs={{0,4},{4,0},{8,12},{12,8},{1,5},{5,1},{9,13},{13,9},{2,6},{6,2},{1... | collective-permute-start | bytes 2359304 | tf_op jit(solution)/shard_map/ppermute | solution.py:103
  189.5 18.9 %collective-permute-start.2 = (bf16[2,3,256,256]{3,2,1,0:T(8,128)(2,1)S(1)}, bf16[2,3,256,256]{3,2,1,0:T(8,128)(2,1)S(1)}, u32[]{:S(2)}, u32[]{:S(2)}) collective-permute-start(bf16[2,3,256,256]{3,2,1,0:T(8,128)(2,1)S(1)} %bitcast.529), channel_id=1, source_target_pairs={{0,4},{4,0},{8,12},{12,8},{1,5},{5,1},{9,13},{13,9},{2,6},{6,2},{1... | collective-permute-start | bytes 2359304 | tf_op jit(solution)/shard_map/ppermute | solution.py:103
  201.1 12.0 %collective-permute-start.21 = (bf16[3,256,256]{2,1,0:T(8,128)(2,1)S(1)}, bf16[3,256,256]{2,1,0:T(8,128)(2,1)S(1)}, u32[]{:S(2)}, u32[]{:S(2)}) collective-permute-start(bf16[3,256,256]{2,1,0:T(8,128)(2,1)S(1)} %fusion.89), channel_id=1, source_target_pairs={{0,8},{4,12},{8,0},{12,4},{1,9},{5,13},{9,1},{13,5},{2,10},{6,14},... | collective-permute-start | bytes 1179656 | tf_op jit(solution)/shard_map/ppermute | solution.py:103
  204.5 20.4 %collective-permute-start.15 = (bf16[3,256,256]{2,1,0:T(8,128)(2,1)}, bf16[3,256,256]{2,1,0:T(8,128)(2,1)}, u32[]{:S(2)}, u32[]{:S(2)}) collective-permute-start(bf16[3,256,256]{2,1,0:T(8,128)(2,1)} %fusion.92), channel_id=1, source_target_pairs={{0,8},{4,12},{8,0},{12,4},{1,9},{5,13},{9,1},{13,5},{2,10},{6,14},... | collective-permute-start | bytes 1179656 | tf_op jit(solution)/shard_map/ppermute | solution.py:103
  206.9 53.0 %collective-permute-start.9 = (bf16[3,256,256]{2,1,0:T(8,128)(2,1)}, bf16[3,256,256]{2,1,0:T(8,128)(2,1)}, u32[]{:S(2)}, u32[]{:S(2)}) collective-permute-start(bf16[3,256,256]{2,1,0:T(8,128)(2,1)} %fusion.95), channel_id=1, source_target_pairs={{0,8},{4,12},{8,0},{12,4},{1,9},{5,13},{9,1},{13,5},{2,10},{6,14},... | collective-permute-start | bytes 1179656 | tf_op jit(solution)/shard_map/ppermute | solution.py:103
  209.3 73.5 %collective-permute-start.3 = (bf16[3,256,256]{2,1,0:T(8,128)(2,1)}, bf16[3,256,256]{2,1,0:T(8,128)(2,1)}, u32[]{:S(2)}, u32[]{:S(2)}) collective-permute-start(bf16[3,256,256]{2,1,0:T(8,128)(2,1)} %fusion.98), channel_id=1, source_target_pairs={{0,8},{4,12},{8,0},{12,4},{1,9},{5,13},{9,1},{13,5},{2,10},{6,14},... | collective-permute-start | bytes 1179656 | tf_op jit(solution)/shard_map/ppermute | solution.py:103
  222.6 18.0 %collective-permute-start.22 = (bf16[256,256]{1,0:T(8,128)(2,1)}, bf16[256,256]{1,0:T(8,128)(2,1)S(1)}, u32[]{:S(2)}, u32[]{:S(2)}) collective-permute-start(bf16[256,256]{1,0:T(8,128)(2,1)} %copy.101), channel_id=1, source_target_pairs={{0,8},{4,12},{8,0},{12,4},{1,9},{5,13},{9,1},{13,5},{2,10},{6,14},... | collective-permute-start | bytes 393224 | tf_op jit(solution)/shard_map/ppermute | solution.py:103
  241.3 4.1 collective-permute-start.23
  252.5 64.5 %reduce-scatter.10.cloned.1.call-start = ((), (), s32[]{:S(2)}) async-start(), calls=%async_computation.7 | async-start | bytes 983040 | tf_op jit(solution)/shard_map/reduce_scatter | solution.py:182
  257.5 6.1 %collective-permute-start.16 = (bf16[256,256]{1,0:T(8,128)(2,1)}, bf16[256,256]{1,0:T(8,128)(2,1)S(1)}, u32[]{:S(2)}, u32[]{:S(2)}) collective-permute-start(bf16[256,256]{1,0:T(8,128)(2,1)} %copy.83), channel_id=1, source_target_pairs={{0,8},{4,12},{8,0},{12,4},{1,9},{5,13},{9,1},{13,5},{2,10},{6,14},... | collective-permute-start | bytes 393224 | tf_op jit(solution)/shard_map/ppermute | solution.py:103
  264.4 4.1 collective-permute-start.17
  275.4 50.1 %reduce-scatter.8.cloned.1.call-start = ((), (), s32[]{:S(2)}) async-start(), calls=%async_computation.6 | async-start | bytes 983040 | tf_op jit(solution)/shard_map/reduce_scatter | solution.py:182
  280.4 6.1 %collective-permute-start.10 = (bf16[256,256]{1,0:T(8,128)(2,1)}, bf16[256,256]{1,0:T(8,128)(2,1)S(1)}, u32[]{:S(2)}, u32[]{:S(2)}) collective-permute-start(bf16[256,256]{1,0:T(8,128)(2,1)} %copy.65), channel_id=1, source_target_pairs={{0,8},{4,12},{8,0},{12,4},{1,9},{5,13},{9,1},{13,5},{2,10},{6,14},... | collective-permute-start | bytes 393224 | tf_op jit(solution)/shard_map/ppermute | solution.py:103
  287.3 5.1 collective-permute-start.11
  299.4 50.9 %reduce-scatter.6.cloned.1.call-start = ((), (), s32[]{:S(2)}) async-start(), calls=%async_computation.5 | async-start | bytes 983040 | tf_op jit(solution)/shard_map/reduce_scatter | solution.py:182
  301.3 6.1 %collective-permute-start.4 = (bf16[256,256]{1,0:T(8,128)(2,1)}, bf16[256,256]{1,0:T(8,128)(2,1)S(1)}, u32[]{:S(2)}, u32[]{:S(2)}) collective-permute-start(bf16[256,256]{1,0:T(8,128)(2,1)} %copy.48), channel_id=1, source_target_pairs={{0,8},{4,12},{8,0},{12,4},{1,9},{5,13},{9,1},{13,5},{2,10},{6,14},... | collective-permute-start | bytes 393224 | tf_op jit(solution)/shard_map/ppermute | solution.py:103
  317.0 246.5 %reduce-scatter.14.cloned.1.call-start = ((), (), s32[]{:S(2)}) async-start(), calls=%async_computation.9 | async-start | bytes 983040 | tf_op jit(solution)/shard_map/reduce_scatter | solution.py:195
  353.1 4.2 collective-permute-start.24
  353.6 4.4 collective-permute-start.43
  355.1 3.6 collective-permute-start.31
  355.8 3.6 collective-permute-start.37
  357.3 3.6 collective-permute-start.25
  386.1 64.1 %collective-permute-start.44 = (bf16[2,64,3072]{2,1,0:T(8,128)(2,1)S(1)}, bf16[2,64,3072]{2,1,0:T(8,128)(2,1)S(1)}, u32[]{:S(2)}, u32[]{:S(2)}) collective-permute-start(bf16[2,64,3072]{2,1,0:T(8,128)(2,1)S(1)} %dynamic-slice_bitcast_fusion), channel_id=1, source_target_pairs={{0,4},{4,0},{8,12},{12,8},{1,5},{5,1},{9,13},{13,9},{2,6},{6,2},{1... | collective-permute-start | bytes 2359304 | tf_op jit(solution)/shard_map/ppermute | solution.py:103
  408.0 43.0 %collective-permute-start.38 = (bf16[2,64,3072]{2,1,0:T(8,128)(2,1)S(1)}, bf16[2,64,3072]{2,1,0:T(8,128)(2,1)S(1)}, u32[]{:S(2)}, u32[]{:S(2)}) collective-permute-start(bf16[2,64,3072]{2,1,0:T(8,128)(2,1)S(1)} %dynamic-slice_bitcast_fusion.1), channel_id=1, source_target_pairs={{0,4},{4,0},{8,12},{12,8},{1,5},{5,1},{9,13},{13,9},{2,6},{6,2},{1... | collective-permute-start | bytes 2359304 | tf_op jit(solution)/shard_map/ppermute | solution.py:103
  429.0 23.6 %collective-permute-start.32 = (bf16[2,64,3072]{2,1,0:T(8,128)(2,1)S(1)}, bf16[2,64,3072]{2,1,0:T(8,128)(2,1)S(1)}, u32[]{:S(2)}, u32[]{:S(2)}) collective-permute-start(bf16[2,64,3072]{2,1,0:T(8,128)(2,1)S(1)} %dynamic-slice_bitcast_fusion.2), channel_id=1, source_target_pairs={{0,4},{4,0},{8,12},{12,8},{1,5},{5,1},{9,13},{13,9},{2,6},{6,2},{1... | collective-permute-start | bytes 2359304 | tf_op jit(solution)/shard_map/ppermute | solution.py:103
  450.1 3.2 collective-permute-start.26
  450.3 12.0 %collective-permute-start.45 = (bf16[64,3072]{1,0:T(8,128)(2,1)S(1)}, bf16[64,3072]{1,0:T(8,128)(2,1)S(1)}, u32[]{:S(2)}, u32[]{:S(2)}) collective-permute-start(bf16[64,3072]{1,0:T(8,128)(2,1)S(1)} %fusion.77), channel_id=1, source_target_pairs={{0,8},{4,12},{8,0},{12,4},{1,9},{5,13},{9,1},{13,5},{2,10},{6,14},... | collective-permute-start | bytes 1179656 | tf_op jit(solution)/shard_map/ppermute | solution.py:103
  451.0 19.7 %collective-permute-start.39 = (bf16[64,3072]{1,0:T(8,128)(2,1)S(1)}, bf16[64,3072]{1,0:T(8,128)(2,1)S(1)}, u32[]{:S(2)}, u32[]{:S(2)}) collective-permute-start(bf16[64,3072]{1,0:T(8,128)(2,1)S(1)} %fusion.80), channel_id=1, source_target_pairs={{0,8},{4,12},{8,0},{12,4},{1,9},{5,13},{9,1},{13,5},{2,10},{6,14},... | collective-permute-start | bytes 1179656 | tf_op jit(solution)/shard_map/ppermute | solution.py:103
  452.7 26.5 %collective-permute-start.33 = (bf16[64,3072]{1,0:T(8,128)(2,1)S(1)}, bf16[64,3072]{1,0:T(8,128)(2,1)S(1)}, u32[]{:S(2)}, u32[]{:S(2)}) collective-permute-start(bf16[64,3072]{1,0:T(8,128)(2,1)S(1)} %fusion.83), channel_id=1, source_target_pairs={{0,8},{4,12},{8,0},{12,4},{1,9},{5,13},{9,1},{13,5},{2,10},{6,14},... | collective-permute-start | bytes 1179656 | tf_op jit(solution)/shard_map/ppermute | solution.py:103
  453.4 33.8 %collective-permute-start.27 = (bf16[64,3072]{1,0:T(8,128)(2,1)S(1)}, bf16[64,3072]{1,0:T(8,128)(2,1)S(1)}, u32[]{:S(2)}, u32[]{:S(2)}) collective-permute-start(bf16[64,3072]{1,0:T(8,128)(2,1)S(1)} %fusion.86), channel_id=1, source_target_pairs={{0,8},{4,12},{8,0},{12,4},{1,9},{5,13},{9,1},{13,5},{2,10},{6,14},... | collective-permute-start | bytes 1179656 | tf_op jit(solution)/shard_map/ppermute | solution.py:103
  488.8 12.1 %collective-permute-start.28 = (bf16[64,3072]{1,0:T(8,128)(2,1)S(1)}, bf16[64,3072]{1,0:T(8,128)(2,1)S(1)}, u32[]{:S(2)}, u32[]{:S(2)}) collective-permute-start(bf16[64,3072]{1,0:T(8,128)(2,1)S(1)} %get-tuple-element.71), channel_id=1, source_target_pairs={{0,8},{4,12},{8,0},{12,4},{1,9},{5,13},{9,1},{13,5},{2,10},{6,14},... | collective-permute-start | bytes 1179656 | tf_op jit(solution)/shard_map/ppermute | solution.py:103
  489.4 19.9 %collective-permute-start.34 = (bf16[64,3072]{1,0:T(8,128)(2,1)S(1)}, bf16[64,3072]{1,0:T(8,128)(2,1)S(1)}, u32[]{:S(2)}, u32[]{:S(2)}) collective-permute-start(bf16[64,3072]{1,0:T(8,128)(2,1)S(1)} %get-tuple-element.72), channel_id=1, source_target_pairs={{0,8},{4,12},{8,0},{12,4},{1,9},{5,13},{9,1},{13,5},{2,10},{6,14},... | collective-permute-start | bytes 1179656 | tf_op jit(solution)/shard_map/ppermute | solution.py:103
  490.9 26.9 %collective-permute-start.40 = (bf16[64,3072]{1,0:T(8,128)(2,1)S(1)}, bf16[64,3072]{1,0:T(8,128)(2,1)S(1)}, u32[]{:S(2)}, u32[]{:S(2)}) collective-permute-start(bf16[64,3072]{1,0:T(8,128)(2,1)S(1)} %get-tuple-element.73), channel_id=1, source_target_pairs={{0,8},{4,12},{8,0},{12,4},{1,9},{5,13},{9,1},{13,5},{2,10},{6,14},... | collective-permute-start | bytes 1179656 | tf_op jit(solution)/shard_map/ppermute | solution.py:103
  491.4 33.4 %collective-permute-start.46 = (bf16[64,3072]{1,0:T(8,128)(2,1)S(1)}, bf16[64,3072]{1,0:T(8,128)(2,1)S(1)}, u32[]{:S(2)}, u32[]{:S(2)}) collective-permute-start(bf16[64,3072]{1,0:T(8,128)(2,1)S(1)} %get-tuple-element.74), channel_id=1, source_target_pairs={{0,8},{4,12},{8,0},{12,4},{1,9},{5,13},{9,1},{13,5},{2,10},{6,14},... | collective-permute-start | bytes 1179656 | tf_op jit(solution)/shard_map/ppermute | solution.py:103
  501.0 26.7 %collective-permute-start.29 = (bf16[2,64,3072]{2,1,0:T(8,128)(2,1)S(1)}, bf16[2,64,3072]{2,1,0:T(8,128)(2,1)S(1)}, u32[]{:S(2)}, u32[]{:S(2)}) collective-permute-start(bf16[2,64,3072]{2,1,0:T(8,128)(2,1)S(1)} %maximum_select_fusion.4), channel_id=1, source_target_pairs={{0,4},{4,0},{8,12},{12,8},{1,5},{5,1},{9,13},{13,9},{2,6},{6,2},{1... | collective-permute-start | bytes 2359304 | tf_op jit(solution)/shard_map/ppermute | solution.py:103
  509.4 16.2 %collective-permute-start.35 = (bf16[2,64,3072]{2,1,0:T(8,128)(2,1)S(1)}, bf16[2,64,3072]{2,1,0:T(8,128)(2,1)S(1)}, u32[]{:S(2)}, u32[]{:S(2)}) collective-permute-start(bf16[2,64,3072]{2,1,0:T(8,128)(2,1)S(1)} %maximum_select_fusion.6), channel_id=1, source_target_pairs={{0,4},{4,0},{8,12},{12,8},{1,5},{5,1},{9,13},{13,9},{2,6},{6,2},{1... | collective-permute-start | bytes 2359304 | tf_op jit(solution)/shard_map/ppermute | solution.py:103
  517.8 8.2 %collective-permute-start.41 = (bf16[2,64,3072]{2,1,0:T(8,128)(2,1)S(1)}, bf16[2,64,3072]{2,1,0:T(8,128)(2,1)S(1)}, u32[]{:S(2)}, u32[]{:S(2)}) collective-permute-start(bf16[2,64,3072]{2,1,0:T(8,128)(2,1)S(1)} %maximum_select_fusion.7), channel_id=1, source_target_pairs={{0,4},{4,0},{8,12},{12,8},{1,5},{5,1},{9,13},{13,9},{2,6},{6,2},{1... | collective-permute-start | bytes 2359304 | tf_op jit(solution)/shard_map/ppermute | solution.py:103
  (58 other events, 957.3 us)
Sparse Core Ops, SparseCore 0:
  252.6 23.0 reduce-scatter.11
  278.1 22.5 reduce-scatter.9
  303.0 22.5 reduce-scatter.7
  327.7 22.5 reduce-scatter.5
  541.4 22.0 reduce-scatter.13

commit v2 on v0

--- a/solution.py
+++ b/solution.py
@@ -20,7 +20,7 @@
     return shaped.reshape(values.shape)
 
 
-def on_device(clip_tokens, modulation, w_qkv, w_out, w_up, up_bias, w_down, guide_num):
+def general_layer(clip_tokens, modulation, w_qkv, w_out, w_up, up_bias, w_down, guide_num):
     branches = modulation.shape[0]
     feat_rows = w_qkv.shape[0]
     head_cols = w_qkv.shape[2]
@@ -95,6 +95,119 @@
     return (resid_mix + mlp_rows).astype(jnp.bfloat16)
 
 
+BF = jnp.bfloat16
+
+
+def swap_row(value, distance):
+    size = lax.axis_size("row")
+    return lax.ppermute(value, "row", [(r, r ^ distance) for r in range(size)])
+
+
+def sum_over_row(value):
+    value = value + swap_row(value, 1)
+    return value + swap_row(value, 2)
+
+
+def scatter_row(partial, axis):
+    me = lax.axis_index("row")
+    half, core = me // 2, me % 2
+    span = partial.shape[axis] // 4
+
+    def piece(index):
+        return lax.dynamic_slice_in_dim(partial, index * span, span, axis)
+
+    far = swap_row(piece((1 - half) * 2 + 1 - core), 1)
+    near = swap_row(piece(half * 2 + 1 - core), 1)
+    away = piece((1 - half) * 2 + core).astype(jnp.float32) + far.astype(jnp.float32)
+    came = swap_row(away.astype(BF), 2)
+    kept = piece(half * 2 + core).astype(jnp.float32) + near.astype(jnp.float32)
+    return kept + came.astype(jnp.float32)
+
+
+def gather_row(value, axis):
+    me = lax.axis_index("row")
+    half, core = me // 2, me % 2
+    beside = swap_row(value, 1)
+    other = swap_row(value, 2)
+    across = swap_row(other, 1)
+
+    def pick(x, c):
+        same = jnp.where(core == c, value, beside)
+        away = jnp.where(core == c, other, across)
+        return jnp.where(half == x, same, away)
+
+    return jnp.concatenate([pick(0, 0), pick(0, 1), pick(1, 0), pick(1, 1)], axis=axis)
+
+
+def moments(values):
+    return jnp.stack([jnp.sum(values, axis=1), jnp.sum(values * values, axis=1)])
+
+
+def apply_norm(values, totals, shift, scale):
+    mean = totals[0] / D
+    variance = totals[1] / D - mean * mean
+    normed = (values - mean[:, None]) * lax.rsqrt(variance + eps)[:, None]
+    branches = shift.shape[0]
+    shaped = normed.reshape(-1, branches, values.shape[1]) * (1.0 + scale[None]) + shift[None]
+    return shaped.reshape(values.shape).astype(BF)
+
+
+def attend(q, k, v):
+    scores = jnp.einsum("qbhd,kbhd->bhqk", q, k, preferred_element_type=jnp.float32)
+    scores = scores / jnp.sqrt(jnp.float32(HEAD_DIM))
+    weights = jnp.exp(scores - jnp.max(scores, axis=-1, keepdims=True))
+    denom = jnp.sum(weights, axis=-1)
+    mixed = jnp.einsum(
+        "bhqk,kbhd->bhqd", weights.astype(BF), v, preferred_element_type=jnp.float32
+    )
+    mixed = mixed / denom[..., None]
+    return mixed.astype(BF).transpose(2, 0, 1, 3)
+
+
+def head_layer(clip_tokens, modulation, w_qkv, w_out, w_up, up_bias, w_down, guide_num):
+    branches = modulation.shape[0]
+    feat_rows, _, head_cols = w_qkv.shape
+    mine = head_cols // 4
+    w_flat = w_qkv.reshape(feat_rows, 3, 4, mine).transpose(0, 2, 1, 3).reshape(feat_rows, -1)
+    x_all = lax.all_gather(clip_tokens, "col", axis=0, tiled=True).astype(jnp.float32)
+    tokens = x_all.shape[0]
+    first = apply_norm(x_all, sum_over_row(moments(x_all)), modulation[:, 0], modulation[:, 1])
+    partial = jnp.dot(first, w_flat, preferred_element_type=jnp.float32).astype(BF)
+    qkv = scatter_row(partial, 1).astype(BF)
+    q, k, v = (
+        qkv[:, i * mine : (i + 1) * mine].reshape(-1, branches, mine // HEAD_DIM, HEAD_DIM)
+        for i in range(3)
+    )
+    att_all = gather_row(attend(q, k, v).reshape(tokens, mine), 1)
+    partial = jnp.dot(att_all, w_out, preferred_element_type=jnp.float32).astype(BF)
+    out = lax.psum_scatter(partial, "col", scatter_dimension=0, tiled=True)
+    x = clip_tokens.astype(jnp.float32)
+    by_branch = x.shape[0] // branches
+    resid = x.reshape(by_branch, branches, feat_rows) + modulation[None, :, 2] * out.astype(
+        jnp.float32
+    ).reshape(by_branch, branches, feat_rows)
+    rows = resid.reshape(x.shape)
+    second = apply_norm(rows, sum_over_row(moments(rows)), modulation[:, 3], modulation[:, 4])
+    second_all = lax.all_gather(second, "col", axis=0, tiled=True)
+    partial = jnp.dot(second_all, w_up, preferred_element_type=jnp.float32).astype(BF)
+    up = scatter_row(partial, 0)
+    act = jax.nn.gelu(up + up_bias[None], approximate=True).astype(BF)
+    down = jnp.dot(gather_row(act, 0), w_down, preferred_element_type=jnp.float32)
+    guide = guide_num.astype(jnp.float32) / 4.0
+    gate = guide[:, None] * modulation[:, 5]
+    total = jnp.sum(down.reshape(-1, branches, feat_rows) * gate[None], axis=1)
+    mlp = lax.psum_scatter(total.astype(BF), "col", scatter_dimension=0, tiled=True)
+    mixed = jnp.sum(resid * guide[None, :, None], axis=1)
+    return (mixed + mlp.astype(jnp.float32)).astype(BF)
+
+
+def on_device(*args):
+    heads_here = args[2].shape[2] // HEAD_DIM
+    if lax.axis_size("row") == 4 and heads_here % 4 == 0:
+        return head_layer(*args)
+    return general_layer(*args)
+
+
 def solution(mesh):
     in_specs = (
         P(("clips", "col"), "row"),

time: 577 us -> 543 us (0.941); the launches traced: 576 us -> 535 us
  waiting for transfers between devices: 402 us -> 334 us
  local copies, waits for them, and re-layouts: 50.5 us -> 84 us
  blocking collectives: 14.7 us -> 0 us
  starting transfers between devices: 0.78 us -> 8.54 us
    ppermute x0 -> x16, waiting for transfers between devices: none -> 134 us  [swap_row(): return lax.ppermute(value, 'row', [(r, r ^ distance) for r in range(size)])]
    reduce_scatter x4 -> x2, waiting for transfers between devices: 183 us -> 68.5 us  [the longest x1 54.9 us: head_layer(): out = lax.psum_scatter(partial, 'col', scatter_dimension=0, tiled=True)]
    all_gather x6 -> x2, waiting for transfers between devices: 219 us -> 131 us  [the longest x1 67.9 us: head_layer(): lax.all_gather(clip_tokens, 'col', axis=0, tiled=True).astype(jnp.float32)]
    psum x2 -> x0, blocking collectives: 14.7 us -> none  [normalize(): lax.psum((jnp.sum(values, axis=1), jnp.sum(values * values, axis=1)), 'row')]
    mul x6, local copies, waits for them, and re-layouts: 9.01 us -> 18.5 us  [the longest x4 15.3 us: apply_norm(): normed.reshape(-1, branches, values.shape[1]) * (1.0 + scale[None])]
    add x4, local copies, waits for them, and re-layouts: 6.03 us -> 15.4 us  [apply_norm(): normed.reshape(-1, branches, values.shape[1]) * (1.0 + scale[None])]
    ppermute x0 -> x16, starting transfers between devices: none -> 8.42 us  [swap_row(): return lax.ppermute(value, 'row', [(r, r ^ distance) for r in range(size)])]
    transpose x0 -> x1, local copies, waits for them, and re-layouts: none -> 7.93 us  [head_layer(): w_qkv.reshape(feat_rows, 3, 4, mine).transpose(0, 2, 1, 3)]
  transfers between devices with their start and end apart: 10 -> 20, of which waited for: 10 -> 14; matrix products, arithmetic and copies ran while one was open for 6% -> 13% of each run, Pallas kernels for 0% -> 0%
where the time goes in v2:
time: 543 us; the launch traced here: 535 us
  waiting for transfers between devices  334 us (62%)
  local copies, waits for them, and re-layouts  84 us (15%)
  matrix products  59 us (11%)
  other arithmetic  35.2 us (6%)
  between operations  13.9 us (3%)
  starting transfers between devices  8.54 us (2%)
    ppermute x16, waiting for transfers between devices, swap_row(): return lax.ppermute(value, 'row', [(r, r ^ distance) for r in range(size)])  134 us
    all_gather x1, waiting for transfers between devices, head_layer(): lax.all_gather(clip_tokens, 'col', axis=0, tiled=True).astype(jnp.float32)  67.9 us
    all_gather x1, waiting for transfers between devices, head_layer(): second_all = lax.all_gather(second, 'col', axis=0, tiled=True)  62.7 us
    reduce_scatter x1, waiting for transfers between devices, head_layer(): out = lax.psum_scatter(partial, 'col', scatter_dimension=0, tiled=True)  54.9 us
    dot_general x1, matrix products, head_layer(): jnp.dot(gather_row(act, 0), w_down, preferred_element_type=jnp.float32)  19.2 us
    dot_general x1, matrix products, head_layer(): jnp.dot(first, w_flat, preferred_element_type=jnp.float32).astype(BF)  19 us
    unnamed x24, local copies, waits for them, and re-layouts  15.9 us
    add x4, local copies, waits for them, and re-layouts, apply_norm(): normed.reshape(-1, branches, values.shape[1]) * (1.0 + scale[None])  15.4 us
  transfers between devices with their start and end apart: 20, of which 14 were waited for; matrix products, arithmetic and copies ran while one was open for 13% of the time, Pallas kernels for 0%

profile of v2, /device:TPU:0, one launch (start us, length us, event | category | flops | bytes accessed | tf_op | source)
XLA Modules:
  0.0 534.9 jit_solution(3436875040953577705)
XLA Ops:
  7.3 67.9 %all-gather.3.cloned.1.call-done = bf16[1024,1536]{1,0:T(8,128)(2,1)} async-done(((bf16[256,1536]{1,0:T(8,128)(2,1)}), bf16[1024,1536]{1,0:T(8,128)(2,1)}) %all-gather.3.cloned.1.call-update) | async-done | bytes 3145744 | tf_op jit(solution)/shard_map/all_gather | solution.py:172
  75.2 2.9 convert_reduce_fusion
  79.3 1.5 collective-permute-start.1
  80.9 12.6 %copy.18 = bf16[1536,3,1024]{0,2,1:T(8,128)(2,1)} copy(bf16[1536,3,1024]{2,0,1:T(8,128)(2,1)} %param.10) | data formatting | bytes 18874368 | tf_op args[2]
  93.6 7.9 %copy.19 = bf16[1536,4,3,256]{0,3,2,1:T(8,128)(2,1)} copy(bf16[1536,4,3,256]{0,3,1,2:T(8,128)(2,1)} %bitcast.49) | data formatting | bytes 18874368 | tf_op jit(solution)/shard_map/transpose | solution.py:171
  101.5 3.5 add.184
  105.0 7.8 %add.185 = f32[1024,1536]{1,0:T(8,128)} reshape(f32[256,4,1536]{2,1,0:T(4,128)} %add.184) | data formatting | bytes 12582912 | tf_op jit(solution)/shard_map/add | solution.py:151
  112.7 3.5 mul.164
  116.2 7.7 %mul.165 = f32[1024,1536]{1,0:T(8,128)} reshape(f32[256,4,1536]{2,1,0:T(4,128)} %mul.164) | data formatting | bytes 12582912 | tf_op jit(solution)/shard_map/mul | solution.py:151
  124.0 19.0 %convolution_convert_fusion.1 = bf16[1024,3072]{1,0:T(8,128)(2,1)} fusion(bf16[1536,3072]{0,1:T(8,128)(2,1)} %bitcast.50, f32[1024,1536]{1,0:T(8,128)} %add.185, f32[1024,1536]{1,0:T(8,128)} %mul.165, bf16[1024,1536]{1,0:T(8,128)(2,1)} %all-gather.3.cloned.1.call-done, f32[1024]{0:T(1024)S(1)} %add_rsqrt_fusion, f32[1024]{0:T(1024)S(1)} %bitcast.66), kind=kOutput, calls=%fused_computation.18 | convolution fusion | flops 9676259328 | bytes 31465472 | tf_op jit(solution)/shard_map/dot_general | solution.py:175
  143.0 3.8 constant_dynamic-slice_fusion.3
  147.3 3.2 collective-permute-done.3
  150.5 3.4 add_convert_fusion.2
  154.5 36.2 %collective-permute-done.4 = bf16[1024,768]{1,0:T(8,128)(2,1)} collective-permute-done((bf16[1024,768]{1,0:T(8,128)(2,1)}, bf16[1024,768]{1,0:T(8,128)(2,1)}, u32[]{:S(2)}, u32[]{:S(2)}) %collective-permute-start.4) | collective-permute-done | bytes 1572896 | tf_op jit(solution)/shard_map/ppermute | solution.py:103
  190.7 2.9 add_convert_fusion.1
  194.8 2.0 reshape.124
  196.8 2.0 reshape.123
  198.8 2.0 reshape.125
  200.7 1.7 multiply_reduce_fusion.1
  206.4 12.9 %collective-permute-done.6 = bf16[1024,256]{1,0:T(8,128)(2,1)} collective-permute-done((bf16[1024,256]{1,0:T(8,128)(2,1)}, bf16[1024,256]{1,0:T(8,128)(2,1)}, u32[]{:S(2)}, u32[]{:S(2)}) %collective-permute-start.6) | collective-permute-done | bytes 524320 | tf_op jit(solution)/shard_map/ppermute | solution.py:103
  219.3 2.2 collective-permute-done.7
  221.6 1.7 broadcast_select_fusion.15
  223.3 4.7 convolution_convert_fusion.2
  229.5 1.8 mul.176
  231.3 54.9 %reduce-scatter.3.cloned.1.call-done = bf16[256,1536]{1,0:T(8,128)(2,1)} async-done(((bf16[1024,1536]{1,0:T(8,128)(2,1)}), bf16[256,1536]{1,0:T(8,128)(2,1)}) %reduce-scatter.3.cloned.1.call-update) | async-done | bytes 786448 | tf_op jit(solution)/shard_map/reduce_scatter | solution.py:183
  286.2 1.6 fusion.47
  289.0 1.5 collective-permute-start.9
  291.9 2.8 add.208
  296.1 2.8 mul.183
  298.9 3.2 add_convert_fusion.3
  302.2 62.7 %all-gather.5.cloned.1.call-done = bf16[1024,1536]{1,0:T(8,128)(2,1)} async-done(((bf16[256,1536]{1,0:T(8,128)(2,1)}), bf16[1024,1536]{1,0:T(8,128)(2,1)}) %all-gather.5.cloned.1.call-update) | async-done | bytes 3145744 | tf_op jit(solution)/shard_map/all_gather | solution.py:191
  364.9 13.6 %convolution_convert_fusion = bf16[1024,3072]{1,0:T(8,128)(2,1)S(1)} fusion(bf16[1024,1536]{1,0:T(8,128)(2,1)} %all-gather.5.cloned.1.call-done, bf16[1536,3072]{1,0:T(8,128)(2,1)} %param.12), kind=kOutput, calls=%fused_computation.17 | convolution fusion | flops 9666822144 | bytes 18874368 | tf_op jit(solution)/shard_map/dot_general | solution.py:192
  378.6 1.6 constant_dynamic-slice_fusion.1
  380.2 1.6 copy-done.4
  382.3 5.1 collective-permute-done.11
  387.4 2.0 add_convert_fusion
  391.0 35.0 %collective-permute-done.12 = bf16[256,3072]{1,0:T(8,128)(2,1)S(1)} collective-permute-done((bf16[256,3072]{1,0:T(8,128)(2,1)S(1)}, bf16[256,3072]{1,0:T(8,128)(2,1)S(1)}, u32[]{:S(2)}, u32[]{:S(2)}) %collective-permute-start.12) | collective-permute-done | bytes 1572896 | tf_op jit(solution)/shard_map/ppermute | solution.py:103
  425.9 3.5 fusion.20
  430.9 34.1 %collective-permute-done.14 = bf16[256,3072]{1,0:T(8,128)(2,1)S(1)} collective-permute-done((bf16[256,3072]{1,0:T(8,128)(2,1)S(1)}, bf16[256,3072]{1,0:T(8,128)(2,1)S(1)}, u32[]{:S(2)}, u32[]{:S(2)}) %collective-permute-start.14) | collective-permute-done | bytes 1572896 | tf_op jit(solution)/shard_map/ppermute | solution.py:103
  465.2 3.3 collective-permute-done.15
  469.1 19.2 %fusion.5 = f32[1024,1536]{1,0:T(8,128)} fusion(bf16[3072,1536]{1,0:T(8,128)(2,1)} %param.14, bf16[256,3072]{1,0:T(8,128)(2,1)S(1)} %get-tuple-element.10, bf16[256,3072]{1,0:T(8,128)(2,1)S(1)} %get-tuple-element.11, bf16[256,3072]{1,0:T(8,128)(2,1)S(1)} %get-tuple-element.12, bf16[256,3072]{1,0:T(8,128)(2,1)S(1)} %get-tuple-element.9), kind=kOutput, calls=%fused_computation.8 | convolution fusion | flops 9688842240 | bytes 22020096 | tf_op jit(solution)/shard_map/dot_general | solution.py:195
  488.3 7.9 %reshape.128 = f32[256,4,1536]{2,1,0:T(4,128)} reshape(f32[1024,1536]{1,0:T(8,128)} %fusion.5) | data formatting | bytes 12582912 | tf_op jit(solution)/shard_map/reshape | solution.py:198
  496.1 8.0 %multiply_reduce_fusion = bf16[256,1536]{1,0:T(8,128)(2,1)} fusion(f32[256,4,1536]{2,1,0:T(4,128)} %reshape.128, f32[4,1536]{1,0:T(4,128)S(1)} %bitcast_multiply_fusion), kind=kLoop, calls=%fused_computation.16 | loop fusion | flops 2752512 | bytes 7102464 | tf_op jit(solution)/shard_map/reduce_sum | solution.py:198
  504.2 2.8 reshape.120
  507.0 2.6 reshape.127
  509.6 3.1 multiply_reduce_fusion.3
  512.7 13.6 %reduce-scatter.5.cloned.1.call-done = bf16[64,1536]{1,0:T(8,128)(2,1)} async-done(((bf16[256,1536]{1,0:T(8,128)(2,1)}), bf16[64,1536]{1,0:T(8,128)(2,1)}) %reduce-scatter.5.cloned.1.call-update) | async-done | bytes 196624 | tf_op jit(solution)/shard_map/reduce_scatter | solution.py:199
  526.3 1.6 add_convert_fusion.4
  (73 shorter events, 18.0 us)
Async XLA Ops:
  6.5 216.7 %copy-start = (bf16[1024,1536]{1,0:T(8,128)(2,1)S(1)}, bf16[1024,1536]{1,0:T(8,128)(2,1)}, u32[]{:S(2)}) copy-start(bf16[1024,1536]{1,0:T(8,128)(2,1)} %param.11) | copy-start | bytes 9437188
  6.5 74.3 %copy-start.8 = (f32[4,6,1536]{2,0,1:T(4,128)S(1)}, f32[4,6,1536]{2,0,1:T(4,128)}, u32[]{:S(2)}) copy-start(f32[4,6,1536]{2,0,1:T(4,128)} %param.9) | copy-start | bytes 442372
  6.5 68.6 %all-gather.3.cloned.1.call-start = ((), (), s32[]{:S(2)}) async-start(), calls=%async_computation.2 | async-start | bytes 3932160 | tf_op jit(solution)/shard_map/all_gather | solution.py:172
  7.3 278.9 %reduce-scatter.3.cloned.1.call-start = ((), (), s32[]{:S(2)}) async-start(), calls=%async_computation.3 | async-start | bytes 3932160 | tf_op jit(solution)/shard_map/reduce_scatter | solution.py:183
  78.1 1.2 collective-permute-start
  79.3 44.6 %collective-permute-start.1 = (f32[2,1024]{1,0:T(2,128)S(1)}, f32[2,1024]{1,0:T(2,128)S(1)}, u32[]{:S(2)}, u32[]{:S(2)}) collective-permute-start(f32[2,1024]{1,0:T(2,128)S(1)} %fusion.46), channel_id=1, source_target_pairs={{0,8},{4,12},{8,0},{12,4},{1,9},{5,13},{9,1},{13,5},{2,10},{6,14},... | collective-permute-start | bytes 24584 | tf_op jit(solution)/shard_map/ppermute | solution.py:103
  80.9 147.2 %copy-start.7 = (f32[4,1536]{1,0:T(4,128)}, f32[4,1536]{1,0:T(4,128)S(1)}, u32[]{:S(2)}) copy-start(f32[4,1536]{1,0:T(4,128)S(1)} %get-tuple-element.27) | copy-start | bytes 73732
  146.8 3.8 collective-permute-start.3
  146.8 7.7 %collective-permute-start.2 = (bf16[1024,768]{1,0:T(8,128)(2,1)}, bf16[1024,768]{1,0:T(8,128)(2,1)}, u32[]{:S(2)}, u32[]{:S(2)}) collective-permute-start(bf16[1024,768]{1,0:T(8,128)(2,1)} %get-tuple-element.15), channel_id=1, source_target_pairs={{0,4},{4,0},{8,12},{12,8},{1,5},{5,1},{9,13},{13,9},{2,6},{6,2},{1... | collective-permute-start | bytes 4718600 | tf_op jit(solution)/shard_map/ppermute | solution.py:103
  153.9 36.8 %collective-permute-start.4 = (bf16[1024,768]{1,0:T(8,128)(2,1)}, bf16[1024,768]{1,0:T(8,128)(2,1)}, u32[]{:S(2)}, u32[]{:S(2)}) collective-permute-start(bf16[1024,768]{1,0:T(8,128)(2,1)} %add_convert_fusion.2), channel_id=1, source_target_pairs={{0,8},{4,12},{8,0},{12,4},{1,9},{5,13},{9,1},{13,5},{2,10},{6,14},... | collective-permute-start | bytes 4718600 | tf_op jit(solution)/shard_map/ppermute | solution.py:103
  200.7 2.1 copy-start.6
  204.2 0.8 copy-start.5
  205.9 13.4 %collective-permute-start.6 = (bf16[1024,256]{1,0:T(8,128)(2,1)}, bf16[1024,256]{1,0:T(8,128)(2,1)}, u32[]{:S(2)}, u32[]{:S(2)}) collective-permute-start(bf16[1024,256]{1,0:T(8,128)(2,1)} %bitcast.48), channel_id=1, source_target_pairs={{0,8},{4,12},{8,0},{12,4},{1,9},{5,13},{9,1},{13,5},{2,10},{6,14},... | collective-permute-start | bytes 1572872 | tf_op jit(solution)/shard_map/ppermute | solution.py:103
  206.4 12.9 %collective-permute-start.5 = (bf16[1024,256]{1,0:T(8,128)(2,1)}, bf16[1024,256]{1,0:T(8,128)(2,1)}, u32[]{:S(2)}, u32[]{:S(2)}) collective-permute-start(bf16[1024,256]{1,0:T(8,128)(2,1)} %bitcast.48), channel_id=1, source_target_pairs={{0,4},{4,0},{8,12},{12,8},{1,5},{5,1},{9,13},{13,9},{2,6},{6,2},{1... | collective-permute-start | bytes 1572872 | tf_op jit(solution)/shard_map/ppermute | solution.py:103
  219.3 2.3 collective-permute-start.7
  228.0 58.1 %copy-start.2 = (bf16[256,1536]{1,0:T(8,128)(2,1)S(1)}, bf16[256,1536]{1,0:T(8,128)(2,1)}, u32[]{:S(2)}) copy-start(bf16[256,1536]{1,0:T(8,128)(2,1)} %param.8) | copy-start | bytes 2359300
  228.1 136.9 %all-gather.5.cloned.1.call-start = ((), (), s32[]{:S(2)}) async-start(), calls=%async_computation.4 | async-start | bytes 3932160 | tf_op jit(solution)/shard_map/all_gather | solution.py:191
  287.8 1.2 collective-permute-start.8
  289.0 9.8 %collective-permute-start.9 = (f32[2,256]{1,0:T(2,128)S(1)}, f32[2,256]{1,0:T(2,128)S(1)}, u32[]{:S(2)}, u32[]{:S(2)}) collective-permute-start(f32[2,256]{1,0:T(2,128)S(1)} %fusion.45), channel_id=1, source_target_pairs={{0,8},{4,12},{8,0},{12,4},{1,9},{5,13},{9,1},{13,5},{2,10},{6,14},... | collective-permute-start | bytes 6152 | tf_op jit(solution)/shard_map/ppermute | solution.py:103
  294.7 4.2 copy-start.3
  302.2 224.1 %reduce-scatter.5.cloned.1.call-start = ((), (), s32[]{:S(2)}) async-start(), calls=%async_computation.5 | async-start | bytes 983040 | tf_op jit(solution)/shard_map/reduce_scatter | solution.py:199
  378.6 3.2 copy-start.4
  381.8 44.1 %copy-start.9 = (f32[3072]{0:T(1024)S(1)}, f32[3072]{0:T(1024)}, u32[]{:S(2)}) copy-start(f32[3072]{0:T(1024)} %param.13) | copy-start | bytes 36868
  381.8 5.6 %collective-permute-start.11 = (bf16[256,3072]{1,0:T(8,128)(2,1)S(1)}, bf16[256,3072]{1,0:T(8,128)(2,1)S(1)}, u32[]{:S(2)}, u32[]{:S(2)}) collective-permute-start(bf16[256,3072]{1,0:T(8,128)(2,1)S(1)} %get-tuple-element.14), channel_id=1, source_target_pairs={{0,4},{4,0},{8,12},{12,8},{1,5},{5,1},{9,13},{13,9},{2,6},{6,2},{1... | collective-permute-start | bytes 4718600 | tf_op jit(solution)/shard_map/ppermute | solution.py:103
  381.8 9.2 %collective-permute-start.10 = (bf16[256,3072]{1,0:T(8,128)(2,1)}, bf16[256,3072]{1,0:T(8,128)(2,1)}, u32[]{:S(2)}, u32[]{:S(2)}) collective-permute-start(bf16[256,3072]{1,0:T(8,128)(2,1)} %get-tuple-element.13), channel_id=1, source_target_pairs={{0,4},{4,0},{8,12},{12,8},{1,5},{5,1},{9,13},{13,9},{2,6},{6,2},{1... | collective-permute-start | bytes 4718600 | tf_op jit(solution)/shard_map/ppermute | solution.py:103
  389.4 36.5 %collective-permute-start.12 = (bf16[256,3072]{1,0:T(8,128)(2,1)S(1)}, bf16[256,3072]{1,0:T(8,128)(2,1)S(1)}, u32[]{:S(2)}, u32[]{:S(2)}) collective-permute-start(bf16[256,3072]{1,0:T(8,128)(2,1)S(1)} %add_convert_fusion), channel_id=1, source_target_pairs={{0,8},{4,12},{8,0},{12,4},{1,9},{5,13},{9,1},{13,5},{2,10},{6,14},... | collective-permute-start | bytes 4718600 | tf_op jit(solution)/shard_map/ppermute | solution.py:103
  391.0 74.1 %copy-start.10 = (s32[4]{0:T(128)S(1)}, s32[4]{0:T(128)}, u32[]{:S(2)}) copy-start(s32[4]{0:T(128)} %param.15) | copy-start | bytes 52
  429.4 35.7 %collective-permute-start.14 = (bf16[256,3072]{1,0:T(8,128)(2,1)S(1)}, bf16[256,3072]{1,0:T(8,128)(2,1)S(1)}, u32[]{:S(2)}, u32[]{:S(2)}) collective-permute-start(bf16[256,3072]{1,0:T(8,128)(2,1)S(1)} %fusion.20), channel_id=1, source_target_pairs={{0,8},{4,12},{8,0},{12,4},{1,9},{5,13},{9,1},{13,5},{2,10},{6,14},... | collective-permute-start | bytes 4718600 | tf_op jit(solution)/shard_map/ppermute | solution.py:103
  430.9 34.2 %collective-permute-start.13 = (bf16[256,3072]{1,0:T(8,128)(2,1)S(1)}, bf16[256,3072]{1,0:T(8,128)(2,1)S(1)}, u32[]{:S(2)}, u32[]{:S(2)}) collective-permute-start(bf16[256,3072]{1,0:T(8,128)(2,1)S(1)} %fusion.20), channel_id=1, source_target_pairs={{0,4},{4,0},{8,12},{12,8},{1,5},{5,1},{9,13},{13,9},{2,6},{6,2},{1... | collective-permute-start | bytes 4718600 | tf_op jit(solution)/shard_map/ppermute | solution.py:103
  465.1 3.4 collective-permute-start.15
  504.2 23.7 %copy-start.1 = (bf16[1024,1536]{1,0:T(8,128)(2,1)S(1)}, bf16[1024,1536]{1,0:T(8,128)(2,1)}, u32[]{:S(2)}) copy-start(bf16[1024,1536]{1,0:T(8,128)(2,1)} %param.11) | copy-start | bytes 9437188
Sparse Core Ops, SparseCore 0:
  8.9 66.1 all-gather.2
  228.2 57.9 reduce-scatter.2
  302.3 62.6 all-gather.4
  504.3 21.9 reduce-scatter.4

commit v3 on v2

--- a/solution.py
+++ b/solution.py
@@ -124,11 +124,27 @@
     return kept + came.astype(jnp.float32)
 
 
-def gather_row(value, axis):
+def shift_col(value, distance):
+    size = lax.axis_size("col")
+    return lax.ppermute(value, "col", [(c, (c + distance) % size) for c in range(size)])
+
+
+def gather_col(value):
+    size = lax.axis_size("col")
+    return jnp.stack([value] + [shift_col(value, k) for k in range(1, size)])
+
+
+def in_order(blocks):
+    size, me = blocks.shape[0], lax.axis_index("col")
+    return jnp.stack(
+        [lax.dynamic_index_in_dim(blocks, (me - k) % size, 0, False) for k in range(size)]
+    )
+
+
+def gather_row(value, other, axis):
     me = lax.axis_index("row")
     half, core = me // 2, me % 2
     beside = swap_row(value, 1)
-    other = swap_row(value, 2)
     across = swap_row(other, 1)
 
     def pick(x, c):
@@ -139,66 +155,116 @@
     return jnp.concatenate([pick(0, 0), pick(0, 1), pick(1, 0), pick(1, 1)], axis=axis)
 
 
-def moments(values):
-    return jnp.stack([jnp.sum(values, axis=1), jnp.sum(values * values, axis=1)])
-
-
 def apply_norm(values, totals, shift, scale):
+    totals = totals.reshape(2, *values.shape[:3])
     mean = totals[0] / D
     variance = totals[1] / D - mean * mean
-    normed = (values - mean[:, None]) * lax.rsqrt(variance + eps)[:, None]
-    branches = shift.shape[0]
-    shaped = normed.reshape(-1, branches, values.shape[1]) * (1.0 + scale[None]) + shift[None]
-    return shaped.reshape(values.shape).astype(BF)
+    normed = (values - mean[..., None]) * lax.rsqrt(variance + eps)[..., None]
+    return (normed * (1.0 + scale[None, :, None]) + shift[None, :, None]).astype(BF)
+
+
+def moments(values):
+    return jnp.stack([jnp.sum(values, axis=-1), jnp.sum(values * values, axis=-1)]).reshape(2, -1)
 
 
 def attend(q, k, v):
-    scores = jnp.einsum("qbhd,kbhd->bhqk", q, k, preferred_element_type=jnp.float32)
+    scores = jnp.einsum("bhqd,bhkd->bhqk", q, k, preferred_element_type=jnp.float32)
     scores = scores / jnp.sqrt(jnp.float32(HEAD_DIM))
     weights = jnp.exp(scores - jnp.max(scores, axis=-1, keepdims=True))
     denom = jnp.sum(weights, axis=-1)
     mixed = jnp.einsum(
-        "bhqk,kbhd->bhqd", weights.astype(BF), v, preferred_element_type=jnp.float32
-    )
-    mixed = mixed / denom[..., None]
-    return mixed.astype(BF).transpose(2, 0, 1, 3)
+        "bhqk,bhkd->bhqd", weights.astype(BF), v, preferred_element_type=jnp.float32
+    )
+    return (mixed / denom[..., None]).astype(BF)
+
+
+GROUPS = 2
 
 
 def head_layer(clip_tokens, modulation, w_qkv, w_out, w_up, up_bias, w_down, guide_num):
     branches = modulation.shape[0]
     feat_rows, _, head_cols = w_qkv.shape
     mine = head_cols // 4
+    heads = mine // HEAD_DIM
+    here = clip_tokens.shape[0] // branches
+    wide = branches // GROUPS
+    cols = lax.axis_size("col")
     w_flat = w_qkv.reshape(feat_rows, 3, 4, mine).transpose(0, 2, 1, 3).reshape(feat_rows, -1)
-    x_all = lax.all_gather(clip_tokens, "col", axis=0, tiled=True).astype(jnp.float32)
-    tokens = x_all.shape[0]
-    first = apply_norm(x_all, sum_over_row(moments(x_all)), modulation[:, 0], modulation[:, 1])
-    partial = jnp.dot(first, w_flat, preferred_element_type=jnp.float32).astype(BF)
-    qkv = scatter_row(partial, 1).astype(BF)
-    q, k, v = (
-        qkv[:, i * mine : (i + 1) * mine].reshape(-1, branches, mine // HEAD_DIM, HEAD_DIM)
-        for i in range(3)
-    )
-    att_all = gather_row(attend(q, k, v).reshape(tokens, mine), 1)
-    partial = jnp.dot(att_all, w_out, preferred_element_type=jnp.float32).astype(BF)
-    out = lax.psum_scatter(partial, "col", scatter_dimension=0, tiled=True)
-    x = clip_tokens.astype(jnp.float32)
-    by_branch = x.shape[0] // branches
-    resid = x.reshape(by_branch, branches, feat_rows) + modulation[None, :, 2] * out.astype(
-        jnp.float32
-    ).reshape(by_branch, branches, feat_rows)
-    rows = resid.reshape(x.shape)
-    second = apply_norm(rows, sum_over_row(moments(rows)), modulation[:, 3], modulation[:, 4])
-    second_all = lax.all_gather(second, "col", axis=0, tiled=True)
-    partial = jnp.dot(second_all, w_up, preferred_element_type=jnp.float32).astype(BF)
-    up = scatter_row(partial, 0)
-    act = jax.nn.gelu(up + up_bias[None], approximate=True).astype(BF)
-    down = jnp.dot(gather_row(act, 0), w_down, preferred_element_type=jnp.float32)
+    by_branch = clip_tokens.reshape(here, branches, feat_rows).transpose(1, 0, 2)
     guide = guide_num.astype(jnp.float32) / 4.0
     gate = guide[:, None] * modulation[:, 5]
-    total = jnp.sum(down.reshape(-1, branches, feat_rows) * gate[None], axis=1)
-    mlp = lax.psum_scatter(total.astype(BF), "col", scatter_dimension=0, tiled=True)
-    mixed = jnp.sum(resid * guide[None, :, None], axis=1)
-    return (mixed + mlp.astype(jnp.float32)).astype(BF)
+    parts = [slice(g * wide, (g + 1) * wide) for g in range(GROUPS)]
+    tokens = cols * wide * here
+    x_parts = [by_branch[p].reshape(wide * here, feat_rows) for p in parts]
+    gathered = [lax.all_gather(x, "col", axis=0, tiled=True) for x in x_parts]
+    gathered[0], w_flat = lax.optimization_barrier((gathered[0], w_flat))
+
+    def project(g):
+        mod = modulation[parts[g]]
+        x_all = gathered[g].astype(jnp.float32).reshape(cols, wide, here, feat_rows)
+        first = apply_norm(x_all, sum_over_row(moments(x_all)), mod[:, 0], mod[:, 1])
+        first = first.reshape(tokens, feat_rows)
+        partial = jnp.dot(first, w_flat, preferred_element_type=jnp.float32).astype(BF)
+        return scatter_row(partial, 1).astype(BF)
+
+    def attention(g, qkv):
+        shaped = qkv.reshape(cols, wide, here, 3, heads, HEAD_DIM).transpose(3, 1, 4, 0, 2, 5)
+        shaped = shaped.reshape(3, wide, heads, cols * here, HEAD_DIM)
+        att = attend(shaped[0], shaped[1], shaped[2])
+        att = att.reshape(wide, heads, cols, here, HEAD_DIM).transpose(2, 0, 3, 1, 4)
+        att = att.reshape(tokens, mine)
+        att_all = gather_row(att, swap_row(att, 2), 1)
+        partial = jnp.dot(att_all, w_out, preferred_element_type=jnp.float32).astype(BF)
+        return lax.psum_scatter(partial, "col", scatter_dimension=0, tiled=True)
+
+    def residual(g, out):
+        mod = modulation[parts[g]]
+        x = x_parts[g].astype(jnp.float32).reshape(1, wide, here, feat_rows)
+        out = out.astype(jnp.float32).reshape(1, wide, here, feat_rows)
+        resid = x + mod[None, :, 2, None] * out
+        second = apply_norm(resid, sum_over_row(moments(resid)), mod[:, 3], mod[:, 4])
+        second = second.reshape(wide * here, feat_rows)
+        mixed = jnp.sum(resid[0] * guide[parts[g]][:, None, None], axis=0)
+        if g < GROUPS - 1:
+            return mixed, gather_col(second).reshape(tokens, feat_rows)
+        return mixed, lax.all_gather(second, "col", axis=0, tiled=True)
+
+    def expand(g, second_all):
+        partial = jnp.dot(second_all, w_up, preferred_element_type=jnp.float32).astype(BF)
+        up = scatter_row(partial, 0)
+        act = jax.nn.gelu(up + up_bias[None], approximate=True).astype(BF)
+        return act, swap_row(act, 2)
+
+    def contract(g, act):
+        down = jnp.dot(gather_row(act[0], act[1], 0), w_down, preferred_element_type=jnp.float32)
+        down = down.reshape(cols, wide, here, feat_rows)
+        down = sum(down[:, b] * gate[parts[g]][b] for b in range(wide))
+        return in_order(down) if g < GROUPS - 1 else down
+
+    every = range(GROUPS)
+    qkv, acts = [], []
+    for g in every:
+        if g:
+            gathered[g], qkv[-1] = lax.optimization_barrier((gathered[g], qkv[-1]))
+        qkv.append(project(g))
+    outs = [attention(g, qkv[g]) for g in every]
+    mixed, seconds = [], []
+    for g in every:
+        out = outs[g]
+        if g:
+            out, seconds[-1] = lax.optimization_barrier((out, seconds[-1]))
+        kept, second = residual(g, out)
+        mixed.append(kept)
+        seconds.append(second)
+    for g in every:
+        second = seconds[g]
+        if g:
+            second, acts[-1] = lax.optimization_barrier((second, acts[-1]))
+        acts.append(expand(g, second))
+    total = sum(contract(g, acts[g]) for g in every)
+    total = total.astype(BF).reshape(cols * here, feat_rows)
+    mlp = lax.psum_scatter(total, "col", scatter_dimension=0, tiled=True)
+    return (sum(mixed) + mlp.astype(jnp.float32)).astype(BF)
 
 
 def on_device(*args):

time: 543 us -> 399 us (0.73)
  waiting for transfers between devices: 334 us -> 213 us
  local copies, waits for them, and re-layouts: 84 us -> 48.3 us
  starting transfers between devices: 8.54 us -> 24.6 us
    all_gather x2 -> x3, waiting for transfers between devices: 131 us -> 21.8 us  [the longest x2 19.2 us: head_layer(): gathered = [lax.all_gather(x, 'col', axis=0, tiled=True) for x in x_parts]]
    ppermute x0 -> x3, waiting for transfers between devices: none -> 43.9 us  [shift_col(): lax.ppermute(value, 'col', [(c, (c + distance) % size) for c in range(siz...]
    reduce_scatter x2 -> x3, waiting for transfers between devices: 68.5 us -> 28.9 us  [the longest x1 28.9 us: head_layer(): mlp = lax.psum_scatter(total, 'col', scatter_dimension=0, tiled=True)]
    mul x6 -> x0, local copies, waits for them, and re-layouts: 18.5 us -> none  [the longest x4 15.3 us: apply_norm(): normed.reshape(-1, branches, values.shape[1]) * (1.0 + scale[None])]
    ppermute x16 -> x32, waiting for transfers between devices: 134 us -> 118 us  [swap_row(): return lax.ppermute(value, 'row', [(r, r ^ distance) for r in range(size)])]
    add x4 -> x0, local copies, waits for them, and re-layouts: 15.4 us -> none  [apply_norm(): normed.reshape(-1, branches, values.shape[1]) * (1.0 + scale[None])]
    ppermute x16 -> x32, starting transfers between devices: 8.42 us -> 20 us  [swap_row(): return lax.ppermute(value, 'row', [(r, r ^ distance) for r in range(size)])]
    reduce_sum x4, other arithmetic: 15.6 us -> 6.07 us  [the longest x2 3.51 us: residual(): mixed = jnp.sum(resid[0] * guide[parts[g]][:, None, None], axis=0)]
  transfers between devices with their start and end apart: 20 -> 41, of which waited for: 14 -> 27; matrix products, arithmetic and copies ran while one was open for 13% -> 26% of each run, Pallas kernels for 0% -> 0%
where the time goes in v3:
time: 399 us; the launch traced here: 394 us
  waiting for transfers between devices  213 us (53%)
  matrix products  57 us (14%)
  local copies, waits for them, and re-layouts  48.3 us (12%)
  other arithmetic  37.1 us (9%)
  starting transfers between devices  24.6 us (6%)
  between operations  14.5 us (4%)
    ppermute x32, waiting for transfers between devices, swap_row(): return lax.ppermute(value, 'row', [(r, r ^ distance) for r in range(size)])  118 us
    ppermute x3, waiting for transfers between devices, shift_col(): lax.ppermute(value, 'col', [(c, (c + distance) % size) for c in range(siz...  43.9 us
    reduce_scatter x1, waiting for transfers between devices, head_layer(): mlp = lax.psum_scatter(total, 'col', scatter_dimension=0, tiled=True)  28.9 us
    ppermute x32, starting transfers between devices, swap_row(): return lax.ppermute(value, 'row', [(r, r ^ distance) for r in range(size)])  20 us
    all_gather x2, waiting for transfers between devices, head_layer(): gathered = [lax.all_gather(x, 'col', axis=0, tiled=True) for x in x_parts]  19.2 us
    dot_general x2, matrix products, project(): jnp.dot(first, w_flat, preferred_element_type=jnp.float32).astype(BF)  18.5 us
    unnamed x55, local copies, waits for them, and re-layouts  18.3 us
    dot_general x2, matrix products, expand(): jnp.dot(second_all, w_up, preferred_element_type=jnp.float32).astype(BF)  17.2 us
  transfers between devices with their start and end apart: 41, of which 27 were waited for; matrix products, arithmetic and copies ran while one was open for 26% of the time, Pallas kernels for 0%

profile of v3, /device:TPU:0, one launch (start us, length us, event | category | flops | bytes accessed | tf_op | source)
XLA Modules:
  0.0 394.1 jit_solution(14099131091044296791)
XLA Ops:
  6.5 2.5 reshape.357
  12.3 12.7 %copy.32 = bf16[1536,3,1024]{0,2,1:T(8,128)(2,1)} copy(bf16[1536,3,1024]{2,0,1:T(8,128)(2,1)} %param.10) | data formatting | bytes 18874368 | tf_op args[2]
  25.0 7.9 %copy.33 = bf16[1536,4,3,256]{0,3,2,1:T(8,128)(2,1)} copy(bf16[1536,4,3,256]{0,3,1,2:T(8,128)(2,1)} %bitcast.146) | data formatting | bytes 18874368 | tf_op jit(solution)/shard_map/transpose | solution.py:192
  32.9 19.2 %all-gather.6.cloned.1.call-done = bf16[512,1536]{1,0:T(8,128)(2,1)} async-done(((bf16[128,1536]{1,0:T(8,128)(2,1)}), bf16[512,1536]{1,0:T(8,128)(2,1)}) %all-gather.6.cloned.1.call-update) | async-done | bytes 1572880 | tf_op jit(solution)/shard_map/all_gather | solution.py:199
  52.2 2.0 convert_reduce_fusion.1
  55.4 1.5 collective-permute-start.1
  59.1 2.7 fusion.4
  61.8 9.3 %convolution_convert_fusion.3 = bf16[512,3072]{1,0:T(8,128)(2,1)S(1)} fusion(bf16[512,1536]{1,0:T(8,128)(2,1)S(1)} %fusion.4, bf16[1536,3072]{0,1:T(8,128)(2,1)} %bitcast.152), kind=kOutput, calls=%fused_computation.9 | convolution fusion | flops 4833411072 | bytes 14155776 | tf_op jit(solution)/shard_map/dot_general | solution.py:207
  73.8 2.1 collective-permute-done.3
  75.9 2.5 add_convert_fusion.5
  79.9 18.4 %collective-permute-done.4 = bf16[512,768]{1,0:T(8,128)(2,1)} collective-permute-done((bf16[512,768]{1,0:T(8,128)(2,1)}, bf16[512,768]{1,0:T(8,128)(2,1)}, u32[]{:S(2)}, u32[]{:S(2)}) %collective-permute-start.4) | collective-permute-done | bytes 786464 | tf_op jit(solution)/shard_map/ppermute | solution.py:103
  98.3 2.8 add_convert_fusion.4
  101.1 2.7 reshape.362
  103.8 1.8 fusion.85
  107.6 1.5 collective-permute-start.9
  112.5 9.1 %convolution_convert_fusion.2 = bf16[512,3072]{1,0:T(8,128)(2,1)S(1)} fusion(bf16[512,1536]{1,0:T(8,128)(2,1)S(1)} %fusion.9, bf16[1536,3072]{0,1:T(8,128)(2,1)} %bitcast.153), kind=kOutput, calls=%fused_computation.8 | convolution fusion | flops 4833411072 | bytes 14155776 | tf_op jit(solution)/shard_map/dot_general | solution.py:207
  124.8 2.0 collective-permute-done.5
  128.4 2.5 add_convert_fusion.3
  132.3 3.0 convolution_convert_fusion.5
  135.4 15.4 %collective-permute-done.12 = bf16[512,768]{1,0:T(8,128)(2,1)} collective-permute-done((bf16[512,768]{1,0:T(8,128)(2,1)}, bf16[512,768]{1,0:T(8,128)(2,1)}, u32[]{:S(2)}, u32[]{:S(2)}) %collective-permute-start.12) | collective-permute-done | bytes 786464 | tf_op jit(solution)/shard_map/ppermute | solution.py:103
  150.8 2.8 add_convert_fusion.2
  153.6 2.9 reshape.367
  156.5 1.8 fusion.86
  159.6 1.5 collective-permute-start.14
  161.1 6.1 %collective-permute-done.14 = bf16[512,256]{1,0:T(8,128)(2,1)S(1)} collective-permute-done((bf16[512,256]{1,0:T(8,128)(2,1)S(1)}, bf16[512,256]{1,0:T(8,128)(2,1)S(1)}, u32[]{:S(2)}, u32[]{:S(2)}) %collective-permute-start.14) | collective-permute-done | bytes 262176 | tf_op jit(solution)/shard_map/ppermute | solution.py:103
  168.8 3.0 convolution_convert_fusion.4
  175.9 1.5 collective-permute-start.17
  177.4 2.1 collective-permute-done.17
  183.2 2.2 collective-permute-start.20
  185.4 17.9 %collective-permute-done.18 = bf16[128,1536]{1,0:T(8,128)(2,1)S(1)} collective-permute-done((bf16[128,1536]{1,0:T(8,128)(2,1)S(1)}, bf16[128,1536]{1,0:T(8,128)(2,1)S(1)}, u32[]{:S(2)}, u32[]{:S(2)}) %collective-permute-start.18) | collective-permute-done | bytes 393248 | tf_op jit(solution)/shard_map/ppermute | solution.py:129
  203.2 26.1 %collective-permute-done.19 = bf16[128,1536]{1,0:T(8,128)(2,1)S(1)} collective-permute-done((bf16[128,1536]{1,0:T(8,128)(2,1)S(1)}, bf16[128,1536]{1,0:T(8,128)(2,1)S(1)}, u32[]{:S(2)}, u32[]{:S(2)}) %collective-permute-start.19) | collective-permute-done | bytes 393248 | tf_op jit(solution)/shard_map/ppermute | solution.py:129
  231.6 2.1 multiply_reduce_fusion.1
  234.0 8.9 %convolution_convert_fusion.1 = bf16[512,3072]{1,0:T(8,128)(2,1)S(1)} fusion(bf16[512,1536]{1,0:T(8,128)(2,1)S(1)} %bitcast.162, bf16[1536,3072]{1,0:T(8,128)(2,1)} %param.12), kind=kOutput, calls=%fused_computation.7 | convolution fusion | flops 4833411072 | bytes 14155776 | tf_op jit(solution)/shard_map/dot_general | solution.py:233
  243.0 1.5 collective-permute-start.22
  250.8 18.5 %collective-permute-done.25 = bf16[128,3072]{1,0:T(8,128)(2,1)S(1)} collective-permute-done((bf16[128,3072]{1,0:T(8,128)(2,1)S(1)}, bf16[128,3072]{1,0:T(8,128)(2,1)S(1)}, u32[]{:S(2)}, u32[]{:S(2)}) %collective-permute-start.25) | collective-permute-done | bytes 786464 | tf_op jit(solution)/shard_map/ppermute | solution.py:103
  269.4 1.9 fusion.33
  272.3 18.0 %collective-permute-done.26 = bf16[128,3072]{1,0:T(8,128)(2,1)S(1)} collective-permute-done((bf16[128,3072]{1,0:T(8,128)(2,1)S(1)}, bf16[128,3072]{1,0:T(8,128)(2,1)S(1)}, u32[]{:S(2)}, u32[]{:S(2)}) %collective-permute-start.26) | collective-permute-done | bytes 786464 | tf_op jit(solution)/shard_map/ppermute | solution.py:103
  291.2 2.6 all-gather.8.cloned.1.call-done
  293.8 8.3 %convolution_convert_fusion = bf16[512,3072]{1,0:T(8,128)(2,1)S(1)} fusion(bf16[512,1536]{1,0:T(8,128)(2,1)} %all-gather.8.cloned.1.call-done, bf16[1536,3072]{1,0:T(8,128)(2,1)} %param.12), kind=kOutput, calls=%fused_computation.6 | convolution fusion | flops 4833411072 | bytes 14155776 | tf_op jit(solution)/shard_map/dot_general | solution.py:233
  307.3 1.5 collective-permute-start.31
  309.3 17.7 %collective-permute-done.31 = bf16[128,3072]{1,0:T(8,128)(2,1)S(1)} collective-permute-done((bf16[128,3072]{1,0:T(8,128)(2,1)S(1)}, bf16[128,3072]{1,0:T(8,128)(2,1)S(1)}, u32[]{:S(2)}, u32[]{:S(2)}) %collective-permute-start.31) | collective-permute-done | bytes 786464 | tf_op jit(solution)/shard_map/ppermute | solution.py:103
  327.8 1.5 collective-permute-start.33
  329.3 8.9 %fusion.10 = f32[512,1536]{1,0:T(8,128)S(1)} fusion(bf16[3072,1536]{1,0:T(8,128)(2,1)} %param.14, bf16[128,3072]{1,0:T(8,128)(2,1)S(1)} %get-tuple-element.42, bf16[128,3072]{1,0:T(8,128)(2,1)S(1)} %get-tuple-element.43, bf16[128,3072]{1,0:T(8,128)(2,1)S(1)} %get-tuple-element.44, bf16[128,3072]{1,0:T(8,128)(2,1)S(1)} %get-tuple-element.41), kind=kOutput, calls=%fused_computation.20 | convolution fusion | flops 4844421120 | bytes 15728640 | tf_op jit(solution)/shard_map/dot_general | solution.py:239
  338.3 8.3 %collective-permute-done.33 = bf16[128,3072]{1,0:T(8,128)(2,1)S(1)} collective-permute-done((bf16[128,3072]{1,0:T(8,128)(2,1)S(1)}, bf16[128,3072]{1,0:T(8,128)(2,1)S(1)}, u32[]{:S(2)}, u32[]{:S(2)}) %collective-permute-start.33) | collective-permute-done | bytes 786464 | tf_op jit(solution)/shard_map/ppermute | solution.py:103
  347.2 1.7 collective-permute-done.34
  349.2 5.0 %fusion.18 = f32[512,1536]{1,0:T(8,128)S(1)} fusion(bf16[3072,1536]{1,0:T(8,128)(2,1)S(1)} %bitcast.204, bf16[128,3072]{1,0:T(8,128)(2,1)S(1)} %get-tuple-element.48, bf16[128,3072]{1,0:T(8,128)(2,1)S(1)} %get-tuple-element.49, bf16[128,3072]{1,0:T(8,128)(2,1)S(1)} %get-tuple-element.50, bf16[128,3072]{1,0:T(8,128)(2,1)S(1)} %get-tuple-element.47), kind=kOutput, calls=%fused_computation.28 | convolution fusion | flops 4844421120 | bytes 15728640 | tf_op jit(solution)/shard_map/dot_general | solution.py:239
  356.0 28.9 %reduce-scatter.8.cloned.1.call-done = bf16[64,1536]{1,0:T(8,128)(2,1)} async-done(((bf16[256,1536]{1,0:T(8,128)(2,1)}), bf16[64,1536]{1,0:T(8,128)(2,1)}) %reduce-scatter.8.cloned.1.call-update) | async-done | bytes 196624 | tf_op jit(solution)/shard_map/reduce_scatter | solution.py:266
  384.9 1.8 add_convert_fusion.8
  (190 shorter events, 52.5 us)
Async XLA Ops:
  6.5 125.8 %copy-start = (bf16[1024,1536]{1,0:T(8,128)(2,1)S(1)}, bf16[1024,1536]{1,0:T(8,128)(2,1)}, u32[]{:S(2)}) copy-start(bf16[1024,1536]{1,0:T(8,128)(2,1)} %param.11) | copy-start | bytes 9437188
  6.5 45.6 %all-gather.6.cloned.1.call-start = ((), (), s32[]{:S(2)}) async-start(), calls=%async_computation.4 | async-start | bytes 1966080 | tf_op jit(solution)/shard_map/all_gather | solution.py:199
  12.2 88.9 %all-gather.4.cloned.1.call-start = ((), (), s32[]{:S(2)}) async-start(), calls=%async_computation.3 | async-start | bytes 1966080 | tf_op jit(solution)/shard_map/all_gather | solution.py:199
  32.9 24.0 %copy-start.15 = (f32[4,6,1536]{2,0,1:T(4,128)S(1)}, f32[4,6,1536]{2,0,1:T(4,128)}, u32[]{:S(2)}) copy-start(f32[4,6,1536]{2,0,1:T(4,128)} %param.9) | copy-start | bytes 442372
  54.2 1.2 collective-permute-start
  54.3 118.9 %reduce-scatter.4.cloned.1.call-start = ((), (), s32[]{:S(2)}) async-start(), calls=%async_computation.5 | async-start | bytes 1966080 | tf_op jit(solution)/shard_map/reduce_scatter | solution.py:218
  55.4 3.7 collective-permute-start.1
  73.3 2.6 collective-permute-start.3
  73.3 6.6 %collective-permute-start.2 = (bf16[512,768]{1,0:T(8,128)(2,1)}, bf16[512,768]{1,0:T(8,128)(2,1)}, u32[]{:S(2)}, u32[]{:S(2)}) collective-permute-start(bf16[512,768]{1,0:T(8,128)(2,1)} %get-tuple-element.57), channel_id=1, source_target_pairs={{0,4},{4,0},{8,12},{12,8},{1,5},{5,1},{9,13},{13,9},{2,6},{6,2},{1... | collective-permute-start | bytes 2359304 | tf_op jit(solution)/shard_map/ppermute | solution.py:103
  78.4 19.9 %collective-permute-start.4 = (bf16[512,768]{1,0:T(8,128)(2,1)}, bf16[512,768]{1,0:T(8,128)(2,1)}, u32[]{:S(2)}, u32[]{:S(2)}) collective-permute-start(bf16[512,768]{1,0:T(8,128)(2,1)} %add_convert_fusion.5), channel_id=1, source_target_pairs={{0,8},{4,12},{8,0},{12,4},{1,9},{5,13},{9,1},{13,5},{2,10},{6,14},... | collective-permute-start | bytes 2359304 | tf_op jit(solution)/shard_map/ppermute | solution.py:103
  106.4 1.2 collective-permute-start.8
  107.6 3.7 collective-permute-start.9
  110.6 13.8 %collective-permute-start.6 = (bf16[512,256]{1,0:T(8,128)(2,1)}, bf16[512,256]{1,0:T(8,128)(2,1)}, u32[]{:S(2)}, u32[]{:S(2)}) collective-permute-start(bf16[512,256]{1,0:T(8,128)(2,1)} %bitcast.145), channel_id=1, source_target_pairs={{0,8},{4,12},{8,0},{12,4},{1,9},{5,13},{9,1},{13,5},{2,10},{6,14},... | collective-permute-start | bytes 786440 | tf_op jit(solution)/shard_map/ppermute | solution.py:103
  123.8 4.6 %collective-permute-start.11 = (bf16[512,768]{1,0:T(8,128)(2,1)}, bf16[512,768]{1,0:T(8,128)(2,1)}, u32[]{:S(2)}, u32[]{:S(2)}) collective-permute-start(bf16[512,768]{1,0:T(8,128)(2,1)} %get-tuple-element.56), channel_id=1, source_target_pairs={{0,4},{4,0},{8,12},{12,8},{1,5},{5,1},{9,13},{13,9},{2,6},{6,2},{1... | collective-permute-start | bytes 2359304 | tf_op jit(solution)/shard_map/ppermute | solution.py:103
  123.8 3.0 collective-permute-start.5
  124.3 2.9 collective-permute-start.7
  124.3 11.0 %collective-permute-start.10 = (bf16[512,768]{1,0:T(8,128)(2,1)}, bf16[512,768]{1,0:T(8,128)(2,1)}, u32[]{:S(2)}, u32[]{:S(2)}) collective-permute-start(bf16[512,768]{1,0:T(8,128)(2,1)} %get-tuple-element.55), channel_id=1, source_target_pairs={{0,4},{4,0},{8,12},{12,8},{1,5},{5,1},{9,13},{13,9},{2,6},{6,2},{1... | collective-permute-start | bytes 2359304 | tf_op jit(solution)/shard_map/ppermute | solution.py:103
  130.9 19.9 %collective-permute-start.12 = (bf16[512,768]{1,0:T(8,128)(2,1)}, bf16[512,768]{1,0:T(8,128)(2,1)}, u32[]{:S(2)}, u32[]{:S(2)}) collective-permute-start(bf16[512,768]{1,0:T(8,128)(2,1)} %add_convert_fusion.3), channel_id=1, source_target_pairs={{0,8},{4,12},{8,0},{12,4},{1,9},{5,13},{9,1},{13,5},{2,10},{6,14},... | collective-permute-start | bytes 2359304 | tf_op jit(solution)/shard_map/ppermute | solution.py:103
  135.3 96.3 %reduce-scatter.6.cloned.1.call-start = ((), (), s32[]{:S(2)}) async-start(), calls=%async_computation.6 | async-start | bytes 1966080 | tf_op jit(solution)/shard_map/reduce_scatter | solution.py:218
  159.6 7.6 %collective-permute-start.14 = (bf16[512,256]{1,0:T(8,128)(2,1)S(1)}, bf16[512,256]{1,0:T(8,128)(2,1)S(1)}, u32[]{:S(2)}, u32[]{:S(2)}) collective-permute-start(bf16[512,256]{1,0:T(8,128)(2,1)S(1)} %bitcast.179), channel_id=1, source_target_pairs={{0,8},{4,12},{8,0},{12,4},{1,9},{5,13},{9,1},{13,5},{2,10},{6,14},... | collective-permute-start | bytes 786440 | tf_op jit(solution)/shard_map/ppermute | solution.py:103
  161.1 6.1 %collective-permute-start.13 = (bf16[512,256]{1,0:T(8,128)(2,1)S(1)}, bf16[512,256]{1,0:T(8,128)(2,1)S(1)}, u32[]{:S(2)}, u32[]{:S(2)}) collective-permute-start(bf16[512,256]{1,0:T(8,128)(2,1)S(1)} %bitcast.180), channel_id=1, source_target_pairs={{0,4},{4,0},{8,12},{12,8},{1,5},{5,1},{9,13},{13,9},{2,6},{6,2},{1... | collective-permute-start | bytes 786440 | tf_op jit(solution)/shard_map/ppermute | solution.py:103
  167.2 1.5 collective-permute-start.15
  171.9 121.9 %all-gather.8.cloned.1.call-start = ((), (), s32[]{:S(2)}) async-start(), calls=%async_computation.7 | async-start | bytes 1966080 | tf_op jit(solution)/shard_map/all_gather | solution.py:230
  174.7 1.2 collective-permute-start.16
  175.9 3.6 collective-permute-start.17
  181.0 22.2 %collective-permute-start.18 = (bf16[128,1536]{1,0:T(8,128)(2,1)S(1)}, bf16[128,1536]{1,0:T(8,128)(2,1)S(1)}, u32[]{:S(2)}, u32[]{:S(2)}) collective-permute-start(bf16[128,1536]{1,0:T(8,128)(2,1)S(1)} %bitcast.163), channel_id=1, source_target_pairs={{0,1},{1,2},{2,3},{3,0},{4,5},{5,6},{6,7},{7,4},{8,9},{9,10},{10,1... | collective-permute-start | bytes 1179656 | tf_op jit(solution)/shard_map/ppermute | solution.py:129
  181.7 47.7 %collective-permute-start.19 = (bf16[128,1536]{1,0:T(8,128)(2,1)S(1)}, bf16[128,1536]{1,0:T(8,128)(2,1)S(1)}, u32[]{:S(2)}, u32[]{:S(2)}) collective-permute-start(bf16[128,1536]{1,0:T(8,128)(2,1)S(1)} %bitcast.164), channel_id=1, source_target_pairs={{0,2},{1,3},{2,0},{3,1},{4,6},{5,7},{6,4},{7,5},{8,10},{9,11},{10,... | collective-permute-start | bytes 1179656 | tf_op jit(solution)/shard_map/ppermute | solution.py:129
  183.2 46.2 %collective-permute-start.20 = (bf16[128,1536]{1,0:T(8,128)(2,1)S(1)}, bf16[128,1536]{1,0:T(8,128)(2,1)S(1)}, u32[]{:S(2)}, u32[]{:S(2)}) collective-permute-start(bf16[128,1536]{1,0:T(8,128)(2,1)S(1)} %bitcast.165), channel_id=1, source_target_pairs={{0,3},{1,0},{2,1},{3,2},{4,7},{5,4},{6,5},{7,6},{8,11},{9,8},{10,9... | collective-permute-start | bytes 1179656 | tf_op jit(solution)/shard_map/ppermute | solution.py:129
  233.9 9.0 %collective-permute-start.21 = (f32[2,128]{1,0:T(2,128)S(1)}, f32[2,128]{1,0:T(2,128)S(1)}, u32[]{:S(2)}, u32[]{:S(2)}) collective-permute-start(f32[2,128]{1,0:T(2,128)S(1)} %pad_maximum_fusion.5), channel_id=1, source_target_pairs={{0,4},{4,0},{8,12},{12,8},{1,5},{5,1},{9,13},{13,9},{2,6},{6,2},{1... | collective-permute-start | bytes 3080 | tf_op jit(solution)/shard_map/ppermute | solution.py:103
  243.0 3.6 collective-permute-start.22
  245.8 2.5 collective-permute-start.24
  246.0 4.8 %collective-permute-start.23 = (bf16[128,3072]{1,0:T(8,128)(2,1)}, bf16[128,3072]{1,0:T(8,128)(2,1)S(1)}, u32[]{:S(2)}, u32[]{:S(2)}) collective-permute-start(bf16[128,3072]{1,0:T(8,128)(2,1)} %get-tuple-element.53), channel_id=1, source_target_pairs={{0,4},{4,0},{8,12},{12,8},{1,5},{5,1},{9,13},{13,9},{2,6},{6,2},{1... | collective-permute-start | bytes 2359304 | tf_op jit(solution)/shard_map/ppermute | solution.py:103
  247.9 21.5 %copy-start.17 = (f32[3072]{0:T(1024)S(1)}, f32[3072]{0:T(1024)}, u32[]{:S(2)}) copy-start(f32[3072]{0:T(1024)} %param.13) | copy-start | bytes 36868
  247.9 137.0 %reduce-scatter.8.cloned.1.call-start = ((), (), s32[]{:S(2)}) async-start(), calls=%async_computation.8 | async-start | bytes 983040 | tf_op jit(solution)/shard_map/reduce_scatter | solution.py:266
  249.7 19.7 %collective-permute-start.25 = (bf16[128,3072]{1,0:T(8,128)(2,1)S(1)}, bf16[128,3072]{1,0:T(8,128)(2,1)S(1)}, u32[]{:S(2)}, u32[]{:S(2)}) collective-permute-start(bf16[128,3072]{1,0:T(8,128)(2,1)S(1)} %add_convert_fusion.1), channel_id=1, source_target_pairs={{0,8},{4,12},{8,0},{12,4},{1,9},{5,13},{9,1},{13,5},{2,10},{6,14},... | collective-permute-start | bytes 2359304 | tf_op jit(solution)/shard_map/ppermute | solution.py:103
  271.3 19.0 %collective-permute-start.26 = (bf16[128,3072]{1,0:T(8,128)(2,1)S(1)}, bf16[128,3072]{1,0:T(8,128)(2,1)S(1)}, u32[]{:S(2)}, u32[]{:S(2)}) collective-permute-start(bf16[128,3072]{1,0:T(8,128)(2,1)S(1)} %fusion.33), channel_id=1, source_target_pairs={{0,8},{4,12},{8,0},{12,4},{1,9},{5,13},{9,1},{13,5},{2,10},{6,14},... | collective-permute-start | bytes 2359304 | tf_op jit(solution)/shard_map/ppermute | solution.py:103
  303.4 2.6 collective-permute-start.30
  304.3 4.6 %collective-permute-start.27 = (bf16[128,3072]{1,0:T(8,128)(2,1)}, bf16[128,3072]{1,0:T(8,128)(2,1)S(1)}, u32[]{:S(2)}, u32[]{:S(2)}) collective-permute-start(bf16[128,3072]{1,0:T(8,128)(2,1)} %copy-done.8), channel_id=1, source_target_pairs={{0,4},{4,0},{8,12},{12,8},{1,5},{5,1},{9,13},{13,9},{2,6},{6,2},{1... | collective-permute-start | bytes 2359304 | tf_op jit(solution)/shard_map/ppermute | solution.py:103
  304.8 4.1 %collective-permute-start.28 = (bf16[128,3072]{1,0:T(8,128)(2,1)}, bf16[128,3072]{1,0:T(8,128)(2,1)S(1)}, u32[]{:S(2)}, u32[]{:S(2)}) collective-permute-start(bf16[128,3072]{1,0:T(8,128)(2,1)} %copy-done.11), channel_id=1, source_target_pairs={{0,4},{4,0},{8,12},{12,8},{1,5},{5,1},{9,13},{13,9},{2,6},{6,2},{1... | collective-permute-start | bytes 2359304 | tf_op jit(solution)/shard_map/ppermute | solution.py:103
  304.9 4.3 %collective-permute-start.29 = (bf16[128,3072]{1,0:T(8,128)(2,1)}, bf16[128,3072]{1,0:T(8,128)(2,1)S(1)}, u32[]{:S(2)}, u32[]{:S(2)}) collective-permute-start(bf16[128,3072]{1,0:T(8,128)(2,1)} %get-tuple-element.51), channel_id=1, source_target_pairs={{0,4},{4,0},{8,12},{12,8},{1,5},{5,1},{9,13},{13,9},{2,6},{6,2},{1... | collective-permute-start | bytes 2359304 | tf_op jit(solution)/shard_map/ppermute | solution.py:103
  307.3 19.6 %collective-permute-start.31 = (bf16[128,3072]{1,0:T(8,128)(2,1)S(1)}, bf16[128,3072]{1,0:T(8,128)(2,1)S(1)}, u32[]{:S(2)}, u32[]{:S(2)}) collective-permute-start(bf16[128,3072]{1,0:T(8,128)(2,1)S(1)} %add_convert_fusion), channel_id=1, source_target_pairs={{0,8},{4,12},{8,0},{12,4},{1,9},{5,13},{9,1},{13,5},{2,10},{6,14},... | collective-permute-start | bytes 2359304 | tf_op jit(solution)/shard_map/ppermute | solution.py:103
  308.9 40.3 %slice-start = ((s8[9437184]{0:T(1024)(128)(4,1)}), s8[4194304]{0:T(1024)(128)(4,1)S(1)}, s32[]{:S(2)}) async-start(s8[9437184]{0:T(1024)(128)(4,1)} %bitcast.203), calls=%async_computation.9 | async-start | bytes 8388608
  327.8 18.8 %collective-permute-start.33 = (bf16[128,3072]{1,0:T(8,128)(2,1)S(1)}, bf16[128,3072]{1,0:T(8,128)(2,1)S(1)}, u32[]{:S(2)}, u32[]{:S(2)}) collective-permute-start(bf16[128,3072]{1,0:T(8,128)(2,1)S(1)} %fusion.41), channel_id=1, source_target_pairs={{0,8},{4,12},{8,0},{12,4},{1,9},{5,13},{9,1},{13,5},{2,10},{6,14},... | collective-permute-start | bytes 2359304 | tf_op jit(solution)/shard_map/ppermute | solution.py:103
  329.3 19.8 %slice-start.1 = ((s8[9437184]{0:T(1024)(128)(4,1)}), s8[4194304]{0:T(1024)(128)(4,1)S(1)}, s32[]{:S(2)}) async-start(s8[9437184]{0:T(1024)(128)(4,1)} %bitcast.203), calls=%async_computation.10 | async-start | bytes 8388608
  329.3 19.9 %slice-start.2 = ((s8[9437184]{0:T(1024)(128)(4,1)}), s8[1048576]{0:T(1024)(128)(4,1)S(1)}, s32[]{:S(2)}) async-start(s8[9437184]{0:T(1024)(128)(4,1)} %bitcast.203), calls=%async_computation.11 | async-start | bytes 2097152
  338.2 8.9 %collective-permute-start.32 = (bf16[128,3072]{1,0:T(8,128)(2,1)S(1)}, bf16[128,3072]{1,0:T(8,128)(2,1)S(1)}, u32[]{:S(2)}, u32[]{:S(2)}) collective-permute-start(bf16[128,3072]{1,0:T(8,128)(2,1)S(1)} %fusion.41), channel_id=1, source_target_pairs={{0,4},{4,0},{8,12},{12,8},{1,5},{5,1},{9,13},{13,9},{2,6},{6,2},{1... | collective-permute-start | bytes 2359304 | tf_op jit(solution)/shard_map/ppermute | solution.py:103
  346.6 2.3 collective-permute-start.34
  354.6 32.2 %copy-start.1 = (bf16[1024,1536]{1,0:T(8,128)(2,1)S(1)}, bf16[1024,1536]{1,0:T(8,128)(2,1)}, u32[]{:S(2)}) copy-start(bf16[1024,1536]{1,0:T(8,128)(2,1)} %param.11) | copy-start | bytes 9437188
  (19 other events, 73.3 us)
Sparse Core Ops, SparseCore 0:
  12.3 39.7 all-gather.5
  54.4 36.0 all-gather.3
  135.4 33.4 reduce-scatter.3
  172.0 58.6 reduce-scatter.5
  248.0 45.7 all-gather.7
  356.2 28.7 reduce-scatter.7

commit v4 on v3

--- a/solution.py
+++ b/solution.py
@@ -225,12 +225,18 @@
         second = apply_norm(resid, sum_over_row(moments(resid)), mod[:, 3], mod[:, 4])
         second = second.reshape(wide * here, feat_rows)
         mixed = jnp.sum(resid[0] * guide[parts[g]][:, None, None], axis=0)
+        if g:
+            seconds[-1], second = lax.optimization_barrier((seconds[-1], second))
         if g < GROUPS - 1:
             return mixed, gather_col(second).reshape(tokens, feat_rows)
         return mixed, lax.all_gather(second, "col", axis=0, tiled=True)
 
     def expand(g, second_all):
         partial = jnp.dot(second_all, w_up, preferred_element_type=jnp.float32).astype(BF)
+        if g:
+            before = acts[g - 1]
+            partial, other = lax.optimization_barrier((partial, before[1]))
+            acts[g - 1] = (before[0], other)
         up = scatter_row(partial, 0)
         act = jax.nn.gelu(up + up_bias[None], approximate=True).astype(BF)
         return act, swap_row(act, 2)
@@ -259,7 +265,8 @@
     for g in every:
         second = seconds[g]
         if g:
-            second, acts[-1] = lax.optimization_barrier((second, acts[-1]))
+            second, act = lax.optimization_barrier((second, acts[-1][0]))
+            acts[-1] = (act, acts[-1][1])
         acts.append(expand(g, second))
     total = sum(contract(g, acts[g]) for g in every)
     total = total.astype(BF).reshape(cols * here, feat_rows)

time: 399 us -> 396 us (level)
  waiting for transfers between devices: 213 us -> 208 us
  other arithmetic: 37.1 us -> 41.5 us
    ppermute x32, waiting for transfers between devices: 118 us -> 103 us  [swap_row(): return lax.ppermute(value, 'row', [(r, r ^ distance) for r in range(size)])]
    all_gather x1, waiting for transfers between devices: 2.57 us -> 16.8 us  [residual(): return (mixed, lax.all_gather(second, 'col', axis=0, tiled=True))]
    reduce_scatter x1, waiting for transfers between devices: 28.9 us -> 24.6 us  [head_layer(): mlp = lax.psum_scatter(total, 'col', scatter_dimension=0, tiled=True)]
    unnamed x55 -> x39, local copies, waits for them, and re-layouts: 18.3 us -> 16.8 us
  transfers between devices with their start and end apart: 41 -> 41, of which waited for: 27 -> 26; matrix products, arithmetic and copies ran while one was open for 26% -> 26% of each run, Pallas kernels for 0% -> 0%
where the time goes in v4:
time: 396 us; the launch traced here: 391 us
  waiting for transfers between devices  208 us (53%)
  matrix products  56.1 us (14%)
  local copies, waits for them, and re-layouts  46.1 us (12%)
  other arithmetic  41.5 us (10%)
  starting transfers between devices  25.4 us (6%)
  between operations  14.4 us (4%)
    ppermute x32, waiting for transfers between devices, swap_row(): return lax.ppermute(value, 'row', [(r, r ^ distance) for r in range(size)])  103 us
    ppermute x3, waiting for transfers between devices, shift_col(): lax.ppermute(value, 'col', [(c, (c + distance) % size) for c in range(siz...  44.1 us
    reduce_scatter x1, waiting for transfers between devices, head_layer(): mlp = lax.psum_scatter(total, 'col', scatter_dimension=0, tiled=True)  24.6 us
    ppermute x32, starting transfers between devices, swap_row(): return lax.ppermute(value, 'row', [(r, r ^ distance) for r in range(size)])  20.8 us
    all_gather x2, waiting for transfers between devices, head_layer(): gathered = [lax.all_gather(x, 'col', axis=0, tiled=True) for x in x_parts]  19.3 us
    dot_general x2, matrix products, project(): jnp.dot(first, w_flat, preferred_element_type=jnp.float32).astype(BF)  18.5 us
    all_gather x1, waiting for transfers between devices, residual(): return (mixed, lax.all_gather(second, 'col', axis=0, tiled=True))  16.8 us
    unnamed x39, local copies, waits for them, and re-layouts  16.8 us
  transfers between devices with their start and end apart: 41, of which 26 were waited for; matrix products, arithmetic and copies ran while one was open for 26% of the time, Pallas kernels for 0%

profile of v4, /device:TPU:0, one launch (start us, length us, event | category | flops | bytes accessed | tf_op | source)
XLA Modules:
  0.0 391.4 jit_solution(15030035954881024947)
XLA Ops:
  6.5 2.5 reshape.357
  12.3 12.6 %copy.32 = bf16[1536,3,1024]{0,2,1:T(8,128)(2,1)} copy(bf16[1536,3,1024]{2,0,1:T(8,128)(2,1)} %param.10) | data formatting | bytes 18874368 | tf_op args[2]
  24.9 8.0 %copy.33 = bf16[1536,4,3,256]{0,3,2,1:T(8,128)(2,1)} copy(bf16[1536,4,3,256]{0,3,1,2:T(8,128)(2,1)} %bitcast.146) | data formatting | bytes 18874368 | tf_op jit(solution)/shard_map/transpose | solution.py:192
  32.9 19.3 %all-gather.6.cloned.1.call-done = bf16[512,1536]{1,0:T(8,128)(2,1)} async-done(((bf16[128,1536]{1,0:T(8,128)(2,1)}), bf16[512,1536]{1,0:T(8,128)(2,1)}) %all-gather.6.cloned.1.call-update) | async-done | bytes 1572880 | tf_op jit(solution)/shard_map/all_gather | solution.py:199
  52.2 2.0 convert_reduce_fusion.1
  59.1 2.7 fusion.4
  61.8 9.3 %convolution_convert_fusion.3 = bf16[512,3072]{1,0:T(8,128)(2,1)S(1)} fusion(bf16[512,1536]{1,0:T(8,128)(2,1)S(1)} %fusion.4, bf16[1536,3072]{0,1:T(8,128)(2,1)} %bitcast.152), kind=kOutput, calls=%fused_computation.9 | convolution fusion | flops 4833411072 | bytes 14155776 | tf_op jit(solution)/shard_map/dot_general | solution.py:207
  73.8 2.1 collective-permute-done.3
  75.9 2.5 add_convert_fusion.5
  79.9 18.4 %collective-permute-done.4 = bf16[512,768]{1,0:T(8,128)(2,1)} collective-permute-done((bf16[512,768]{1,0:T(8,128)(2,1)}, bf16[512,768]{1,0:T(8,128)(2,1)}, u32[]{:S(2)}, u32[]{:S(2)}) %collective-permute-start.4) | collective-permute-done | bytes 786464 | tf_op jit(solution)/shard_map/ppermute | solution.py:103
  98.3 2.8 add_convert_fusion.4
  101.1 2.7 reshape.362
  103.8 1.8 fusion.85
  112.5 9.1 %convolution_convert_fusion.2 = bf16[512,3072]{1,0:T(8,128)(2,1)S(1)} fusion(bf16[512,1536]{1,0:T(8,128)(2,1)S(1)} %fusion.9, bf16[1536,3072]{0,1:T(8,128)(2,1)} %bitcast.153), kind=kOutput, calls=%fused_computation.8 | convolution fusion | flops 4833411072 | bytes 14155776 | tf_op jit(solution)/shard_map/dot_general | solution.py:207
  124.8 2.0 collective-permute-done.5
  128.4 2.4 add_convert_fusion.3
  132.3 3.0 convolution_convert_fusion.5
  135.3 15.4 %collective-permute-done.12 = bf16[512,768]{1,0:T(8,128)(2,1)} collective-permute-done((bf16[512,768]{1,0:T(8,128)(2,1)}, bf16[512,768]{1,0:T(8,128)(2,1)}, u32[]{:S(2)}, u32[]{:S(2)}) %collective-permute-start.12) | collective-permute-done | bytes 786464 | tf_op jit(solution)/shard_map/ppermute | solution.py:103
  150.7 2.8 add_convert_fusion.2
  153.5 2.9 reshape.367
  156.4 1.8 fusion.86
  159.5 1.5 collective-permute-start.14
  161.0 6.0 %collective-permute-done.14 = bf16[512,256]{1,0:T(8,128)(2,1)S(1)} collective-permute-done((bf16[512,256]{1,0:T(8,128)(2,1)S(1)}, bf16[512,256]{1,0:T(8,128)(2,1)S(1)}, u32[]{:S(2)}, u32[]{:S(2)}) %collective-permute-start.14) | collective-permute-done | bytes 262176 | tf_op jit(solution)/shard_map/ppermute | solution.py:103
  168.7 3.0 convolution_convert_fusion.4
  175.6 1.5 collective-permute-start.17
  177.1 2.1 collective-permute-done.17
  182.9 2.2 collective-permute-start.20
  185.1 17.8 %collective-permute-done.18 = bf16[128,1536]{1,0:T(8,128)(2,1)S(1)} collective-permute-done((bf16[128,1536]{1,0:T(8,128)(2,1)S(1)}, bf16[128,1536]{1,0:T(8,128)(2,1)S(1)}, u32[]{:S(2)}, u32[]{:S(2)}) %collective-permute-start.18) | collective-permute-done | bytes 393248 | tf_op jit(solution)/shard_map/ppermute | solution.py:129
  203.0 26.3 %collective-permute-done.19 = bf16[128,1536]{1,0:T(8,128)(2,1)S(1)} collective-permute-done((bf16[128,1536]{1,0:T(8,128)(2,1)S(1)}, bf16[128,1536]{1,0:T(8,128)(2,1)S(1)}, u32[]{:S(2)}, u32[]{:S(2)}) %collective-permute-start.19) | collective-permute-done | bytes 393248 | tf_op jit(solution)/shard_map/ppermute | solution.py:129
  230.6 2.1 multiply_reduce_fusion.1
  234.1 1.5 collective-permute-start.22
  235.6 2.1 collective-permute-done.22
  237.9 2.1 add_convert_fusion.6
  240.0 8.1 %convolution_convert_fusion.1 = bf16[512,3072]{1,0:T(8,128)(2,1)S(1)} fusion(bf16[512,1536]{1,0:T(8,128)(2,1)} %bitcast.162, bf16[1536,3072]{1,0:T(8,128)(2,1)} %param.12), kind=kOutput, calls=%fused_computation.7 | convolution fusion | flops 4833411072 | bytes 14155776 | tf_op jit(solution)/shard_map/dot_general | solution.py:235
  250.0 2.0 collective-permute-done.24
  252.0 2.2 add_convert_fusion.1
  255.7 18.4 %collective-permute-done.25 = bf16[128,3072]{1,0:T(8,128)(2,1)} collective-permute-done((bf16[128,3072]{1,0:T(8,128)(2,1)}, bf16[128,3072]{1,0:T(8,128)(2,1)}, u32[]{:S(2)}, u32[]{:S(2)}) %collective-permute-start.25) | collective-permute-done | bytes 786464 | tf_op jit(solution)/shard_map/ppermute | solution.py:103
  274.1 3.1 fusion.33
  278.6 16.8 %all-gather.8.cloned.1.call-done = bf16[512,1536]{1,0:T(8,128)(2,1)} async-done(((bf16[128,1536]{1,0:T(8,128)(2,1)}), bf16[512,1536]{1,0:T(8,128)(2,1)}) %all-gather.8.cloned.1.call-update) | async-done | bytes 1572880 | tf_op jit(solution)/shard_map/all_gather | solution.py:232
  295.4 8.3 %convolution_convert_fusion = bf16[512,3072]{1,0:T(8,128)(2,1)S(1)} fusion(bf16[512,1536]{1,0:T(8,128)(2,1)} %all-gather.8.cloned.1.call-done, bf16[1536,3072]{1,0:T(8,128)(2,1)} %param.12), kind=kOutput, calls=%fused_computation.6 | convolution fusion | flops 4833411072 | bytes 14155776 | tf_op jit(solution)/shard_map/dot_general | solution.py:235
  310.6 1.8 broadcast_select_fusion.15
  312.4 16.3 %collective-permute-done.31 = bf16[128,3072]{1,0:T(8,128)(2,1)S(1)} collective-permute-done((bf16[128,3072]{1,0:T(8,128)(2,1)S(1)}, bf16[128,3072]{1,0:T(8,128)(2,1)S(1)}, u32[]{:S(2)}, u32[]{:S(2)}) %collective-permute-start.31) | collective-permute-done | bytes 786464 | tf_op jit(solution)/shard_map/ppermute | solution.py:103
  331.0 8.9 %fusion.10 = f32[512,1536]{1,0:T(8,128)S(1)} fusion(bf16[3072,1536]{1,0:T(8,128)(2,1)} %param.14, bf16[128,3072]{1,0:T(8,128)(2,1)S(1)} %get-tuple-element.48, bf16[128,3072]{1,0:T(8,128)(2,1)S(1)} %get-tuple-element.49, bf16[128,3072]{1,0:T(8,128)(2,1)S(1)} %get-tuple-element.50, bf16[128,3072]{1,0:T(8,128)(2,1)S(1)} %get-tuple-element.47), kind=kOutput, calls=%fused_computation.20 | convolution fusion | flops 4844421120 | bytes 15728640 | tf_op jit(solution)/shard_map/dot_general | solution.py:245
  340.0 8.3 %collective-permute-done.33 = bf16[128,3072]{1,0:T(8,128)(2,1)S(1)} collective-permute-done((bf16[128,3072]{1,0:T(8,128)(2,1)S(1)}, bf16[128,3072]{1,0:T(8,128)(2,1)S(1)}, u32[]{:S(2)}, u32[]{:S(2)}) %collective-permute-start.33) | collective-permute-done | bytes 786464 | tf_op jit(solution)/shard_map/ppermute | solution.py:103
  348.8 1.7 collective-permute-done.34
  350.9 5.0 %fusion.18 = f32[512,1536]{1,0:T(8,128)S(1)} fusion(bf16[3072,1536]{1,0:T(8,128)(2,1)S(1)} %bitcast.204, bf16[128,3072]{1,0:T(8,128)(2,1)S(1)} %get-tuple-element.54, bf16[128,3072]{1,0:T(8,128)(2,1)S(1)} %get-tuple-element.55, bf16[128,3072]{1,0:T(8,128)(2,1)S(1)} %get-tuple-element.56, bf16[128,3072]{1,0:T(8,128)(2,1)S(1)} %get-tuple-element.53), kind=kOutput, calls=%fused_computation.28 | convolution fusion | flops 4844421120 | bytes 15728640 | tf_op jit(solution)/shard_map/dot_general | solution.py:245
  357.7 24.6 %reduce-scatter.8.cloned.1.call-done = bf16[64,1536]{1,0:T(8,128)(2,1)} async-done(((bf16[256,1536]{1,0:T(8,128)(2,1)}), bf16[64,1536]{1,0:T(8,128)(2,1)}) %reduce-scatter.8.cloned.1.call-update) | async-done | bytes 196624 | tf_op jit(solution)/shard_map/reduce_scatter | solution.py:273
  382.2 1.8 add_convert_fusion.8
  (174 shorter events, 55.2 us)
Async XLA Ops:
  6.5 125.7 %copy-start = (bf16[1024,1536]{1,0:T(8,128)(2,1)S(1)}, bf16[1024,1536]{1,0:T(8,128)(2,1)}, u32[]{:S(2)}) copy-start(bf16[1024,1536]{1,0:T(8,128)(2,1)} %param.11) | copy-start | bytes 9437188
  6.5 45.6 %all-gather.6.cloned.1.call-start = ((), (), s32[]{:S(2)}) async-start(), calls=%async_computation.4 | async-start | bytes 1966080 | tf_op jit(solution)/shard_map/all_gather | solution.py:199
  12.2 88.9 %all-gather.4.cloned.1.call-start = ((), (), s32[]{:S(2)}) async-start(), calls=%async_computation.3 | async-start | bytes 1966080 | tf_op jit(solution)/shard_map/all_gather | solution.py:199
  32.9 24.1 %copy-start.7 = (f32[4,6,1536]{2,0,1:T(4,128)S(1)}, f32[4,6,1536]{2,0,1:T(4,128)}, u32[]{:S(2)}) copy-start(f32[4,6,1536]{2,0,1:T(4,128)} %param.9) | copy-start | bytes 442372
  54.2 1.2 collective-permute-start
  54.3 118.1 %reduce-scatter.4.cloned.1.call-start = ((), (), s32[]{:S(2)}) async-start(), calls=%async_computation.5 | async-start | bytes 1966080 | tf_op jit(solution)/shard_map/reduce_scatter | solution.py:218
  55.4 3.7 collective-permute-start.1
  73.3 2.6 collective-permute-start.3
  73.3 6.6 %collective-permute-start.2 = (bf16[512,768]{1,0:T(8,128)(2,1)}, bf16[512,768]{1,0:T(8,128)(2,1)}, u32[]{:S(2)}, u32[]{:S(2)}) collective-permute-start(bf16[512,768]{1,0:T(8,128)(2,1)} %get-tuple-element.63), channel_id=1, source_target_pairs={{0,4},{4,0},{8,12},{12,8},{1,5},{5,1},{9,13},{13,9},{2,6},{6,2},{1... | collective-permute-start | bytes 2359304 | tf_op jit(solution)/shard_map/ppermute | solution.py:103
  78.4 19.9 %collective-permute-start.4 = (bf16[512,768]{1,0:T(8,128)(2,1)}, bf16[512,768]{1,0:T(8,128)(2,1)}, u32[]{:S(2)}, u32[]{:S(2)}) collective-permute-start(bf16[512,768]{1,0:T(8,128)(2,1)} %add_convert_fusion.5), channel_id=1, source_target_pairs={{0,8},{4,12},{8,0},{12,4},{1,9},{5,13},{9,1},{13,5},{2,10},{6,14},... | collective-permute-start | bytes 2359304 | tf_op jit(solution)/shard_map/ppermute | solution.py:103
  106.3 1.2 collective-permute-start.8
  107.6 3.7 collective-permute-start.9
  110.5 13.8 %collective-permute-start.6 = (bf16[512,256]{1,0:T(8,128)(2,1)}, bf16[512,256]{1,0:T(8,128)(2,1)}, u32[]{:S(2)}, u32[]{:S(2)}) collective-permute-start(bf16[512,256]{1,0:T(8,128)(2,1)} %bitcast.145), channel_id=1, source_target_pairs={{0,8},{4,12},{8,0},{12,4},{1,9},{5,13},{9,1},{13,5},{2,10},{6,14},... | collective-permute-start | bytes 786440 | tf_op jit(solution)/shard_map/ppermute | solution.py:103
  123.8 4.6 %collective-permute-start.11 = (bf16[512,768]{1,0:T(8,128)(2,1)}, bf16[512,768]{1,0:T(8,128)(2,1)}, u32[]{:S(2)}, u32[]{:S(2)}) collective-permute-start(bf16[512,768]{1,0:T(8,128)(2,1)} %get-tuple-element.62), channel_id=1, source_target_pairs={{0,4},{4,0},{8,12},{12,8},{1,5},{5,1},{9,13},{13,9},{2,6},{6,2},{1... | collective-permute-start | bytes 2359304 | tf_op jit(solution)/shard_map/ppermute | solution.py:103
  123.8 3.0 collective-permute-start.5
  124.3 2.9 collective-permute-start.7
  124.3 11.0 %collective-permute-start.10 = (bf16[512,768]{1,0:T(8,128)(2,1)}, bf16[512,768]{1,0:T(8,128)(2,1)}, u32[]{:S(2)}, u32[]{:S(2)}) collective-permute-start(bf16[512,768]{1,0:T(8,128)(2,1)} %get-tuple-element.61), channel_id=1, source_target_pairs={{0,4},{4,0},{8,12},{12,8},{1,5},{5,1},{9,13},{13,9},{2,6},{6,2},{1... | collective-permute-start | bytes 2359304 | tf_op jit(solution)/shard_map/ppermute | solution.py:103
  130.8 19.9 %collective-permute-start.12 = (bf16[512,768]{1,0:T(8,128)(2,1)}, bf16[512,768]{1,0:T(8,128)(2,1)}, u32[]{:S(2)}, u32[]{:S(2)}) collective-permute-start(bf16[512,768]{1,0:T(8,128)(2,1)} %add_convert_fusion.3), channel_id=1, source_target_pairs={{0,8},{4,12},{8,0},{12,4},{1,9},{5,13},{9,1},{13,5},{2,10},{6,14},... | collective-permute-start | bytes 2359304 | tf_op jit(solution)/shard_map/ppermute | solution.py:103
  135.3 95.3 %reduce-scatter.6.cloned.1.call-start = ((), (), s32[]{:S(2)}) async-start(), calls=%async_computation.6 | async-start | bytes 1966080 | tf_op jit(solution)/shard_map/reduce_scatter | solution.py:218
  159.5 7.6 %collective-permute-start.14 = (bf16[512,256]{1,0:T(8,128)(2,1)S(1)}, bf16[512,256]{1,0:T(8,128)(2,1)S(1)}, u32[]{:S(2)}, u32[]{:S(2)}) collective-permute-start(bf16[512,256]{1,0:T(8,128)(2,1)S(1)} %bitcast.179), channel_id=1, source_target_pairs={{0,8},{4,12},{8,0},{12,4},{1,9},{5,13},{9,1},{13,5},{2,10},{6,14},... | collective-permute-start | bytes 786440 | tf_op jit(solution)/shard_map/ppermute | solution.py:103
  161.0 6.1 %collective-permute-start.13 = (bf16[512,256]{1,0:T(8,128)(2,1)S(1)}, bf16[512,256]{1,0:T(8,128)(2,1)S(1)}, u32[]{:S(2)}, u32[]{:S(2)}) collective-permute-start(bf16[512,256]{1,0:T(8,128)(2,1)S(1)} %bitcast.180), channel_id=1, source_target_pairs={{0,4},{4,0},{8,12},{12,8},{1,5},{5,1},{9,13},{13,9},{2,6},{6,2},{1... | collective-permute-start | bytes 786440 | tf_op jit(solution)/shard_map/ppermute | solution.py:103
  167.1 1.5 collective-permute-start.15
  171.7 123.7 %all-gather.8.cloned.1.call-start = ((), (), s32[]{:S(2)}) async-start(), calls=%async_computation.7 | async-start | bytes 1966080 | tf_op jit(solution)/shard_map/all_gather | solution.py:232
  174.4 1.2 collective-permute-start.16
  175.6 3.6 collective-permute-start.17
  180.7 22.2 %collective-permute-start.18 = (bf16[128,1536]{1,0:T(8,128)(2,1)S(1)}, bf16[128,1536]{1,0:T(8,128)(2,1)S(1)}, u32[]{:S(2)}, u32[]{:S(2)}) collective-permute-start(bf16[128,1536]{1,0:T(8,128)(2,1)S(1)} %bitcast.163), channel_id=1, source_target_pairs={{0,1},{1,2},{2,3},{3,0},{4,5},{5,6},{6,7},{7,4},{8,9},{9,10},{10,1... | collective-permute-start | bytes 1179656 | tf_op jit(solution)/shard_map/ppermute | solution.py:129
  181.4 47.8 %collective-permute-start.19 = (bf16[128,1536]{1,0:T(8,128)(2,1)S(1)}, bf16[128,1536]{1,0:T(8,128)(2,1)S(1)}, u32[]{:S(2)}, u32[]{:S(2)}) collective-permute-start(bf16[128,1536]{1,0:T(8,128)(2,1)S(1)} %bitcast.164), channel_id=1, source_target_pairs={{0,2},{1,3},{2,0},{3,1},{4,6},{5,7},{6,4},{7,5},{8,10},{9,11},{10,... | collective-permute-start | bytes 1179656 | tf_op jit(solution)/shard_map/ppermute | solution.py:129
  182.9 46.3 %collective-permute-start.20 = (bf16[128,1536]{1,0:T(8,128)(2,1)S(1)}, bf16[128,1536]{1,0:T(8,128)(2,1)S(1)}, u32[]{:S(2)}, u32[]{:S(2)}) collective-permute-start(bf16[128,1536]{1,0:T(8,128)(2,1)S(1)} %bitcast.165), channel_id=1, source_target_pairs={{0,3},{1,0},{2,1},{3,2},{4,7},{5,4},{6,5},{7,6},{8,11},{9,8},{10,9... | collective-permute-start | bytes 1179656 | tf_op jit(solution)/shard_map/ppermute | solution.py:129
  232.9 1.2 collective-permute-start.21
  234.1 3.6 collective-permute-start.22
  249.3 24.8 %copy-start.9 = (f32[3072]{0:T(1024)S(1)}, f32[3072]{0:T(1024)}, u32[]{:S(2)}) copy-start(f32[3072]{0:T(1024)} %param.13) | copy-start | bytes 36868
  249.3 2.6 collective-permute-start.24
  249.4 132.9 %reduce-scatter.8.cloned.1.call-start = ((), (), s32[]{:S(2)}) async-start(), calls=%async_computation.8 | async-start | bytes 983040 | tf_op jit(solution)/shard_map/reduce_scatter | solution.py:273
  249.4 6.2 %collective-permute-start.23 = (bf16[128,3072]{1,0:T(8,128)(2,1)}, bf16[128,3072]{1,0:T(8,128)(2,1)}, u32[]{:S(2)}, u32[]{:S(2)}) collective-permute-start(bf16[128,3072]{1,0:T(8,128)(2,1)} %get-tuple-element.59), channel_id=1, source_target_pairs={{0,4},{4,0},{8,12},{12,8},{1,5},{5,1},{9,13},{13,9},{2,6},{6,2},{1... | collective-permute-start | bytes 2359304 | tf_op jit(solution)/shard_map/ppermute | solution.py:103
  254.2 19.9 %collective-permute-start.25 = (bf16[128,3072]{1,0:T(8,128)(2,1)}, bf16[128,3072]{1,0:T(8,128)(2,1)}, u32[]{:S(2)}, u32[]{:S(2)}) collective-permute-start(bf16[128,3072]{1,0:T(8,128)(2,1)} %add_convert_fusion.1), channel_id=1, source_target_pairs={{0,8},{4,12},{8,0},{12,4},{1,9},{5,13},{9,1},{13,5},{2,10},{6,14},... | collective-permute-start | bytes 2359304 | tf_op jit(solution)/shard_map/ppermute | solution.py:103
  277.1 26.6 %collective-permute-start.27 = (bf16[128,3072]{1,0:T(8,128)(2,1)}, bf16[128,3072]{1,0:T(8,128)(2,1)}, u32[]{:S(2)}, u32[]{:S(2)}) collective-permute-start(bf16[128,3072]{1,0:T(8,128)(2,1)} %fusion.33), channel_id=1, source_target_pairs={{0,8},{4,12},{8,0},{12,4},{1,9},{5,13},{9,1},{13,5},{2,10},{6,14},... | collective-permute-start | bytes 2359304 | tf_op jit(solution)/shard_map/ppermute | solution.py:103
  305.0 2.6 collective-permute-start.30
  305.9 4.7 %collective-permute-start.26 = (bf16[128,3072]{1,0:T(8,128)(2,1)}, bf16[128,3072]{1,0:T(8,128)(2,1)S(1)}, u32[]{:S(2)}, u32[]{:S(2)}) collective-permute-start(bf16[128,3072]{1,0:T(8,128)(2,1)} %fusion.33), channel_id=1, source_target_pairs={{0,4},{4,0},{8,12},{12,8},{1,5},{5,1},{9,13},{13,9},{2,6},{6,2},{1... | collective-permute-start | bytes 2359304 | tf_op jit(solution)/shard_map/ppermute | solution.py:103
  306.4 4.2 %collective-permute-start.28 = (bf16[128,3072]{1,0:T(8,128)(2,1)}, bf16[128,3072]{1,0:T(8,128)(2,1)S(1)}, u32[]{:S(2)}, u32[]{:S(2)}) collective-permute-start(bf16[128,3072]{1,0:T(8,128)(2,1)} %collective-permute-done.27), channel_id=1, source_target_pairs={{0,4},{4,0},{8,12},{12,8},{1,5},{5,1},{9,13},{13,9},{2,6},{6,2},{1... | collective-permute-start | bytes 2359304 | tf_op jit(solution)/shard_map/ppermute | solution.py:103
  306.5 5.9 %collective-permute-start.29 = (bf16[128,3072]{1,0:T(8,128)(2,1)}, bf16[128,3072]{1,0:T(8,128)(2,1)S(1)}, u32[]{:S(2)}, u32[]{:S(2)}) collective-permute-start(bf16[128,3072]{1,0:T(8,128)(2,1)} %get-tuple-element.57), channel_id=1, source_target_pairs={{0,4},{4,0},{8,12},{12,8},{1,5},{5,1},{9,13},{13,9},{2,6},{6,2},{1... | collective-permute-start | bytes 2359304 | tf_op jit(solution)/shard_map/ppermute | solution.py:103
  309.0 19.6 %collective-permute-start.31 = (bf16[128,3072]{1,0:T(8,128)(2,1)S(1)}, bf16[128,3072]{1,0:T(8,128)(2,1)S(1)}, u32[]{:S(2)}, u32[]{:S(2)}) collective-permute-start(bf16[128,3072]{1,0:T(8,128)(2,1)S(1)} %add_convert_fusion), channel_id=1, source_target_pairs={{0,8},{4,12},{8,0},{12,4},{1,9},{5,13},{9,1},{13,5},{2,10},{6,14},... | collective-permute-start | bytes 2359304 | tf_op jit(solution)/shard_map/ppermute | solution.py:103
  310.6 40.3 %slice-start = ((s8[9437184]{0:T(1024)(128)(4,1)}), s8[4194304]{0:T(1024)(128)(4,1)S(1)}, s32[]{:S(2)}) async-start(s8[9437184]{0:T(1024)(128)(4,1)} %bitcast.203), calls=%async_computation.9 | async-start | bytes 8388608
  329.5 18.8 %collective-permute-start.33 = (bf16[128,3072]{1,0:T(8,128)(2,1)S(1)}, bf16[128,3072]{1,0:T(8,128)(2,1)S(1)}, u32[]{:S(2)}, u32[]{:S(2)}) collective-permute-start(bf16[128,3072]{1,0:T(8,128)(2,1)S(1)} %fusion.41), channel_id=1, source_target_pairs={{0,8},{4,12},{8,0},{12,4},{1,9},{5,13},{9,1},{13,5},{2,10},{6,14},... | collective-permute-start | bytes 2359304 | tf_op jit(solution)/shard_map/ppermute | solution.py:103
  331.0 19.8 %slice-start.1 = ((s8[9437184]{0:T(1024)(128)(4,1)}), s8[4194304]{0:T(1024)(128)(4,1)S(1)}, s32[]{:S(2)}) async-start(s8[9437184]{0:T(1024)(128)(4,1)} %bitcast.203), calls=%async_computation.10 | async-start | bytes 8388608
  331.0 19.9 %slice-start.2 = ((s8[9437184]{0:T(1024)(128)(4,1)}), s8[1048576]{0:T(1024)(128)(4,1)S(1)}, s32[]{:S(2)}) async-start(s8[9437184]{0:T(1024)(128)(4,1)} %bitcast.203), calls=%async_computation.11 | async-start | bytes 2097152
  339.9 8.9 %collective-permute-start.32 = (bf16[128,3072]{1,0:T(8,128)(2,1)S(1)}, bf16[128,3072]{1,0:T(8,128)(2,1)S(1)}, u32[]{:S(2)}, u32[]{:S(2)}) collective-permute-start(bf16[128,3072]{1,0:T(8,128)(2,1)S(1)} %fusion.41), channel_id=1, source_target_pairs={{0,4},{4,0},{8,12},{12,8},{1,5},{5,1},{9,13},{13,9},{2,6},{6,2},{1... | collective-permute-start | bytes 2359304 | tf_op jit(solution)/shard_map/ppermute | solution.py:103
  348.3 2.3 collective-permute-start.34
  356.3 27.8 %copy-start.1 = (bf16[1024,1536]{1,0:T(8,128)(2,1)S(1)}, bf16[1024,1536]{1,0:T(8,128)(2,1)}, u32[]{:S(2)}) copy-start(bf16[1024,1536]{1,0:T(8,128)(2,1)} %param.11) | copy-start | bytes 9437188
  (11 other events, 42.9 us)
Sparse Core Ops, SparseCore 0:
  12.4 39.7 all-gather.5
  54.4 36.0 all-gather.3
  135.4 33.4 reduce-scatter.3
  171.9 58.6 reduce-scatter.5
  249.5 45.9 all-gather.7
  357.8 24.4 reduce-scatter.7
